TPU v7x, 256 devices: a whole 4x4x8 slice. The times are simulated.
256 devices in a mesh: segment: 4 (over z_hi, core), expert: 64 (over z_lo, x, y).
Axes of the slice: x: 4, y: 4, z: 8 (z_hi: 2, z_lo: 4; z = z_hi * 4 + z_lo), core: 2. Of those that a mesh axis runs over, the one named last changes fastest.
Arguments:
- act_a: bfloat16 [4, 1536, 2048], P('segment', 'expert'), may hold values from -6 to 6
- route_a1: int32 [4, 1536, 8], P('segment', 'expert'), may hold values from 0 to 63, all different within a row; in each aligned block of 24 rows (0 to 23, 24 to 47, ..., all dimensions but the last counted through in order) at most 4 rows name the same one
- gate_a1: float32 [4, 1536, 8], P('segment', 'expert'), may hold values from 0.1 to 0.5
- act_b1: bfloat16 [4, 1536, 2048], P('segment', 'expert'), may hold values from -6 to 6
- route_b1: int32 [4, 1536, 8], P('segment', 'expert'), may hold values from 0 to 63, all different within a row; in each aligned block of 24 rows (0 to 23, 24 to 47, ..., all dimensions but the last counted through in order) at most 4 rows name the same one
- gate_b1: float32 [4, 1536, 8], P('segment', 'expert'), may hold values from 0.1 to 0.5
- grad_b1: bfloat16 [4, 1536, 2048], P('segment', 'expert'), may hold values from -6 to 6
- act_b2: bfloat16 [4, 1536, 2048], P('segment', 'expert'), may hold values from -6 to 6
- route_a2: int32 [4, 1536, 8], P('segment', 'expert'), may hold values from 0 to 63, all different within a row; in each aligned block of 24 rows (0 to 23, 24 to 47, ..., all dimensions but the last counted through in order) at most 4 rows name the same one
- gate_a2: float32 [4, 1536, 8], P('segment', 'expert'), may hold values from 0.1 to 0.5
- route_b2: int32 [4, 1536, 8], P('segment', 'expert'), may hold values from 0 to 63, all different within a row; in each aligned block of 24 rows (0 to 23, 24 to 47, ..., all dimensions but the last counted through in order) at most 4 rows name the same one
- gate_b2: float32 [4, 1536, 8], P('segment', 'expert'), may hold values from 0.1 to 0.5
- enter_a: bfloat16 [1536, 2048], P('expert'), may hold values from -6 to 6
- enter_grad: bfloat16 [1536, 2048], P('expert'), may hold values from -6 to 6
- w_gate: bfloat16 [4, 64, 2048, 768], P('segment', 'expert'), may hold values from -0.125 to 0.125
- w_up: bfloat16 [4, 64, 2048, 768], P('segment', 'expert'), may hold values from -0.125 to 0.125
- w_down: bfloat16 [4, 64, 768, 2048], P('segment', 'expert'), may hold values from -0.21875 to 0.21875
Outputs:
- fwd_one: bfloat16 [4, 1536, 2048], P('segment', 'expert')
- grad_one: bfloat16 [4, 1536, 2048], P('segment', 'expert')
- fwd_two: bfloat16 [4, 1536, 2048], P('segment', 'expert')
- grad_two: bfloat16 [4, 1536, 2048], P('segment', 'expert')
Inputs may be any that keep to these rules, and one draw needn't show every extreme that they name: `route_a1`: in each row the 8 experts differ; in the 24 rows of one device of one section no expert is named more than 4 times, a bound that some block reaches. `route_b1`: as for route_a1. `route_a2`: as for route_a1. `route_b2`: as for route_a1.
All inputs are finite; a program needn't handle non-finite values.
Results may differ from a plain program's by a relative error of at most 0.0085.
Values may be sent and summed in bfloat16 or wider, within the bound.
No kernel may reach another device: no remote copies, remote signals or barrier semaphores. Data moves between devices by JAX's collectives and lax.ppermute only.
A program may use at most 128 MiB of HBM per device.

v0:
```python
import functools

import jax
import jax.numpy as jnp
from jax import lax
from jax.experimental import pallas as pl
from jax.experimental.pallas import tpu as pltpu
from jax.sharding import Mesh, PartitionSpec as P

TOP = 8
ROWS = 24
NZ = 4
SIDE = 4
PLANE = 16
CAP = 4
SLOTS = PLANE * NZ * CAP
TOKENS = NZ * ROWS
LANES = 128
PIECES = 4
THIRDS = 3
F32 = jnp.float32
BF16 = jnp.bfloat16


def dot(a, b):
    return jnp.dot(a, b, preferred_element_type=F32)


def dot_t(a, b):
    return lax.dot_general(a, b, (((1,), (1,)), ((), ())), preferred_element_type=F32)


def iota(shape, dim):
    return lax.broadcasted_iota(jnp.int32, shape, dim)


def block_of(token):
    return sum((token >= ROWS * k).astype(jnp.int32) for k in range(1, NZ + 1))


def thirds(value):
    high = value.astype(BF16).astype(F32)
    rest = value - high
    middle = rest.astype(BF16).astype(F32)
    return high, middle, rest - middle


def pack_kernel(act, grad, ra1, rb1, ra2, rb2, ga1, gb1, ga2, gb2, out, meta):
    width = act.shape[1]
    out[:, 0:width] = act[...]
    out[:, width : 2 * width] = grad[...]
    meta[...] = jnp.zeros_like(meta)
    arrays = [r[...].astype(F32) for r in (ra1, rb1, ra2, rb2)]
    for g in (ga1, gb1, ga2, gb2):
        arrays.extend(thirds(g[...]))
    for i, block in enumerate(arrays):
        meta[TOP * i : TOP * (i + 1), 0:ROWS] = block
    out[:, 2 * width : 2 * width + LANES] = meta[...].T[0:ROWS].astype(BF16)


def meta_of(pieces):
    parts = [p[...].astype(F32) for p in pieces]
    parts.append(jnp.zeros((LANES - TOKENS, LANES), F32))
    return jnp.concatenate(parts, axis=0).T


def ranks_of(meta, place, i):
    lane = iota((TOP, LANES), 1)
    zpos = place // PLANE
    route = meta[TOP * i : TOP * (i + 1)] - (zpos * PLANE).astype(F32)
    route = jnp.where(lane < TOKENS, route, -1.0)
    expert = iota((PLANE, LANES), 0).astype(F32)
    hits = [(route[j : j + 1, :] == expert).astype(F32) for j in range(TOP)]
    named = sum(hits[1:], hits[0])
    before = iota((LANES, LANES), 0)
    later = iota((LANES, LANES), 1)
    earlier = (block_of(before) == block_of(later)) & (before < later)
    rank = dot(named.astype(BF16), earlier.astype(F32).astype(BF16))
    return named * (rank + 1.0), hits


def select_of(rank):
    row = iota((SLOTS, LANES), 0)
    col = iota((SLOTS, LANES), 1)
    target = jnp.where((row // CAP) % NZ == block_of(col), row % CAP + 1, -1).astype(F32)
    copies = iota((SLOTS, PLANE), 0) // (NZ * CAP) == iota((SLOTS, PLANE), 1)
    spread = dot(copies.astype(F32).astype(BF16), rank.astype(BF16))
    return (spread == target).astype(F32).astype(BF16)


def stack(pieces):
    parts = [p[...].astype(F32) for p in pieces]
    parts.append(jnp.zeros((LANES - TOKENS, parts[0].shape[1]), F32))
    return jnp.concatenate(parts, axis=0).astype(BF16)


def first_kernel(place, m0, m1, m2, m3, p0, p1, p2, p3, out, select):
    @pl.when(pl.program_id(0) == 0)
    def _():
        rank, _ = ranks_of(meta_of((m0, m1, m2, m3)), place[0], 1)
        select[...] = select_of(rank)

    out[...] = dot(select[...], stack((p0, p1, p2, p3))).astype(BF16)


def plan_kernel(place, m0, m1, m2, m3, select, weight):
    meta = meta_of((m0, m1, m2, m3))
    copies = iota((PLANE, SLOTS), 1) // (NZ * CAP) == iota((PLANE, SLOTS), 0)
    copies = copies.astype(F32).astype(BF16)
    row = iota((LANES, SLOTS), 1)
    col = iota((LANES, SLOTS), 0)
    target = jnp.where((row // CAP) % NZ == block_of(col), row % CAP + 1, -1).astype(F32)
    for i in range(4):
        rank, hits = ranks_of(meta, place[0], i)
        if i != 1:
            select[i - i // 2] = select_of(rank)
        mask = dot(rank.T.astype(BF16), copies) == target
        for part in range(3):
            first = TOP * (4 + 3 * i + part)
            gate = meta[first : first + TOP]
            named = sum(hits[j] * gate[j : j + 1, :] for j in range(TOP))
            spread = dot(named.T.astype(BF16), copies)
            weight[i, part] = jnp.where(mask, spread, 0.0).astype(BF16)


def dispatch_kernel(select, p0, p1, p2, p3, out):
    out[...] = dot(select[0], stack((p0, p1, p2, p3))).astype(BF16)


def combine_kernel(weight, rows, own, b1, b2, b3):
    values = rows[...]
    total = sum(dot(weight[0, part], values) for part in range(3))
    own[...] = total[0:ROWS]
    for k, out in ((1, b1), (2, b2), (3, b3)):
        out[...] = total[ROWS * k : ROWS * (k + 1)].astype(BF16)


def sum_of(own, b1, b2, b3):
    total = own[...] + b1[...].astype(F32) + b2[...].astype(F32) + b3[...].astype(F32)
    return total.astype(BF16)


def sum_kernel(own, b1, b2, b3, out):
    out[...] = sum_of(own, b1, b2, b3)


def pass_kernel(edge, own, b1, b2, b3, enter, out, onward):
    total = sum_of(own, b1, b2, b3)
    out[...] = total
    onward[...] = total

    @pl.when(edge[0] == 1)
    def _():
        onward[...] = enter[...]


def part(ref, k):
    size = ref.shape[0] // PIECES
    return ref.at[pl.ds(pl.multiple_of(size * k, size), size)]


def fetch(pair, sems, k):
    source, target = pair
    return pltpu.make_async_copy(part(source, k), part(target, k), sems.at[k])


def column(ref, k):
    size = ref.shape[1] // PIECES
    return ref.at[:, pl.ds(pl.multiple_of(size * k, size), size)]


def loop(body, count=PIECES):
    lax.fori_loop(0, count, lambda k, _: body(k), None)


def begin(whole, pieces, sems, semp):
    for i, (source, target) in enumerate(whole):
        pltpu.make_async_copy(source, target, sems.at[i]).start()
    for k in range(PIECES):
        for i, pair in enumerate(pieces):
            fetch(pair, semp.at[i], k).start()


def pre_activations(x, gate, up, semp, gate_pre, up_pre):
    gate_pre[...] = jnp.zeros_like(gate_pre)
    up_pre[...] = jnp.zeros_like(up_pre)

    def step(k):
        for i, (pair, total) in enumerate(((gate, gate_pre), (up, up_pre))):
            fetch(pair, semp.at[i], k).wait()
            total[...] += dot(column(x, k)[...], part(pair[1], k)[...])

    loop(step)


def send(out, result, sent, k):
    return pltpu.make_async_copy(column(out, k), column(result, k), sent.at[k])


def forward_kernel(rows, w_gate, w_up, w_down, result, *scratch):
    x, gate_mat, up_mat, down_mat, out, gate_pre, up_pre, hidden, sems, semp, sent = scratch
    whole = ((rows, x), (w_down, down_mat))
    gate, up = (w_gate, gate_mat), (w_up, up_mat)
    begin(whole[:1], (gate, up), sems, semp)
    pltpu.make_async_copy(w_down, down_mat, sems.at[1]).start()
    pltpu.make_async_copy(rows, x, sems.at[0]).wait()
    pre_activations(x, gate, up, semp, gate_pre, up_pre)
    hidden[...] = (jax.nn.silu(gate_pre[...]) * up_pre[...]).astype(BF16)
    pltpu.make_async_copy(w_down, down_mat, sems.at[1]).wait()

    def step(k):
        column(out, k)[...] = dot(hidden[...], column(down_mat, k)[...]).astype(BF16)
        send(out, result, sent, k).start()

    loop(step)
    for k in range(PIECES):
        send(out, result, sent, k).wait()


def backward_kernel(place, xs, cs, w_gate, w_up, w_down, result, *scratch):
    x, c, gate_mat, up_mat, down_mat, out = scratch[:6]
    gate_pre, up_pre, d_gate, d_upper, sems, semp, sent = scratch[6:]
    width = x.shape[1]
    gate, up = (w_gate, gate_mat), (w_up, up_mat)
    rows = pltpu.make_async_copy(xs.at[:, pl.ds(0, width)], x, sems.at[0])
    cots = pltpu.make_async_copy(cs.at[:, pl.ds(place * width, width)], c, sems.at[1])
    downs = pltpu.make_async_copy(w_down, down_mat, sems.at[2])
    rows.start()
    begin((), (gate, up), sems, semp)
    cots.start()
    downs.start()
    rows.wait()
    pre_activations(x, gate, up, semp, gate_pre, up_pre)
    cots.wait()
    downs.wait()
    size = down_mat.shape[0] // THIRDS

    def inner(k):
        cols = pl.ds(pl.multiple_of(size * k, size), size)
        d_hidden = dot_t(c[...], down_mat[cols, :])
        g, u = gate_pre[:, cols], up_pre[:, cols]
        sigma = jax.nn.sigmoid(g)
        d_gate[:, cols] = (d_hidden * u * sigma * (1.0 + g * (1.0 - sigma))).astype(BF16)
        d_upper[:, cols] = (d_hidden * g * sigma).astype(BF16)

    loop(inner, THIRDS)

    def step(k):
        total = dot_t(d_gate[...], part(gate_mat, k)[...])
        total = total + dot_t(d_upper[...], part(up_mat, k)[...])
        column(out, k)[...] = total.astype(BF16)
        send(out, result, sent, k).start()

    loop(step)
    for k in range(PIECES):
        send(out, result, sent, k).wait()


SMEM = pl.BlockSpec(memory_space=pltpu.SMEM)
ANY = pl.BlockSpec(memory_space=pl.ANY)
HBM = pl.BlockSpec(memory_space=pltpu.HBM)


def spec(shape, index):
    return pl.BlockSpec(shape, index)


def whole(array):
    zeros = (0,) * len(array.shape)
    return pl.BlockSpec(tuple(array.shape), lambda *_: zeros)


def shaped(*shape, dtype=BF16):
    return jax.ShapeDtypeStruct(shape, dtype)


def after(value, *others):
    return lax.optimization_barrier((value,) + others)[0]


def call(
    line, kernel, name, grid, in_specs, args, out_specs, outs, scratch=(), flops=0, room=16
):
    if line:
        args = (after(args[0], line[-1]),) + tuple(args[1:])
    moved = sum(a.size * a.dtype.itemsize for a in args)
    moved += sum(o.size * o.dtype.itemsize for o in outs)
    results = pl.pallas_call(
        kernel,
        name=name,
        grid=grid,
        in_specs=in_specs,
        out_specs=out_specs,
        out_shape=outs,
        scratch_shapes=scratch,
        cost_estimate=pl.CostEstimate(flops=flops, bytes_accessed=moved, transcendentals=0),
        compiler_params=pltpu.CompilerParams(
            vmem_limit_bytes=room << 20, dimension_semantics=("arbitrary",) * len(grid)
        ),
    )(*args)
    line.append(results[0])
    return results


def shift(block, axis, k):
    size = lax.axis_size(axis)
    return lax.ppermute(block, axis, [(i, (i + k) % size) for i in range(size)])


def to_section(block, step, k):
    sections = lax.axis_size("segment")
    route = [
        (s * NZ + i, ((s + step) % sections) * NZ + (i + k) % NZ)
        for s in range(sections)
        for i in range(NZ)
    ]
    return lax.ppermute(block, ("segment", "z"), route)


def gather_z(block):
    return (block,) + tuple(shift(block, "z", k) for k in (1, 2, 3))


def plane(rows):
    block = rows.reshape(PLANE, NZ * CAP, rows.shape[-1])
    return lax.all_to_all(block, ("x", "y"), split_axis=0, concat_axis=0, tiled=True).reshape(
        rows.shape
    )


def shards(
    act_a,
    route_a1,
    gate_a1,
    act_b1,
    route_b1,
    gate_b1,
    grad_b1,
    act_b2,
    route_a2,
    gate_a2,
    route_b2,
    gate_b2,
    enter_a,
    enter_grad,
    w_gate,
    w_up,
    w_down,
):
    width = act_a.shape[2]
    hidden = w_gate.shape[3]
    mats = (w_gate[0, 0], w_up[0, 0], w_down[0, 0])
    place = lax.axis_index(("z", "x", "y")).astype(jnp.int32)[None]
    section = lax.axis_index("segment")
    last = lax.axis_size("segment") - 1
    half = width // 2
    buffer = shaped(SLOTS, width)
    slot_specs = [spec((SLOTS, half), lambda i: (0, i))]
    row_specs = [spec((ROWS, half), lambda i: (0, i))] * NZ

    line = []
    run = functools.partial(call, line)
    args = (act_b1[0], grad_b1[0]) + tuple(
        v[0].T
        for v in (route_a1, route_b1, route_a2, route_b2, gate_a1, gate_b1, gate_a2, gate_b2)
    )
    packed = shaped(ROWS, 2 * width + LANES)
    (head,) = run(
        pack_kernel,
        "pack",
        (1,),
        [whole(a) for a in args],
        args,
        [whole(packed)],
        [packed],
        [pltpu.VMEM((LANES, LANES), F32)],
        room=60,
    )
    head = gather_z(head)
    meta_specs = [spec((ROWS, LANES), lambda i: (0, 2 * width // LANES))] * NZ
    (send_b1,) = run(
        first_kernel,
        "first",
        (4,),
        [SMEM] + meta_specs + row_specs,
        (place,) + head + head,
        slot_specs,
        [shaped(SLOTS, 2 * width)],
        [pltpu.VMEM((SLOTS, LANES), BF16)],
    )
    plans = [shaped(3, SLOTS, LANES), shaped(4, 3, LANES, SLOTS)]
    select, weight = run(
        plan_kernel,
        "plan",
        (1,),
        [SMEM] + meta_specs,
        (place,) + head,
        [whole(p) for p in plans],
        plans,
    )

    def dispatch(i, pieces):
        size = pieces[0].shape[1]
        (rows,) = run(
            dispatch_kernel,
            "dispatch",
            (size // half,),
            [spec((1, SLOTS, LANES), lambda _: (i - i // 2, 0, 0))]
            + [spec((ROWS, half), lambda j: (0, j))] * NZ,
            (select,) + tuple(pieces),
            slot_specs,
            [shaped(SLOTS, size)],
        )
        return rows

    def combine(i, rows):
        parts = run(
            combine_kernel,
            "combine",
            (2,),
            [spec((1, 3, LANES, SLOTS), lambda _: (i, 0, 0, 0))] + slot_specs,
            (weight, rows),
            row_specs,
            [shaped(ROWS, width, dtype=F32)] + [shaped(ROWS, width)] * 3,
        )
        return [parts[0]] + [shift(parts[k], "z", -k) for k in (1, 2, 3)]

    def finish(parts):
        out = shaped(ROWS, width)
        (total,) = run(
            sum_kernel, "sum", (1,), [whole(p) for p in parts], parts, [whole(out)], [out]
        )
        return total

    def onward(parts, edge, enter, step):
        out = shaped(ROWS, width)
        args = (edge.astype(jnp.int32)[None],) + tuple(parts) + (enter,)
        total, moving = run(
            pass_kernel,
            "pass",
            (1,),
            [SMEM] + [whole(a) for a in args[1:]],
            args,
            [whole(out)] * 2,
            [out] * 2,
        )
        return total, [to_section(moving, step, k) for k in range(NZ)]

    rows_buffer = pltpu.VMEM((SLOTS, width), BF16)
    wide_buffer = pltpu.VMEM((SLOTS, hidden), F32)
    thin_buffer = pltpu.VMEM((SLOTS, hidden), BF16)
    mat_buffers = [pltpu.VMEM(m.shape, BF16) for m in mats]

    def forward(rows):
        (out,) = run(
            forward_kernel,
            "forward",
            (),
            [ANY] + [HBM] * 3,
            (rows,) + mats,
            [ANY],
            [buffer],
            [rows_buffer]
            + mat_buffers
            + [
                rows_buffer,
                wide_buffer,
                wide_buffer,
                thin_buffer,
                pltpu.SemaphoreType.DMA((2,)),
                pltpu.SemaphoreType.DMA((2, PIECES)),
                pltpu.SemaphoreType.DMA((PIECES,)),
            ],
            6 * SLOTS * width * hidden,
            room=60,
        )
        return out

    def backward(x, c, column):
        (out,) = run(
            functools.partial(backward_kernel, column),
            "backward",
            (),
            [ANY] * 2 + [HBM] * 3,
            (x, c) + mats,
            [ANY],
            [shaped(SLOTS, width)],
            [rows_buffer, rows_buffer]
            + mat_buffers
            + [
                rows_buffer,
                wide_buffer,
                wide_buffer,
                thin_buffer,
                thin_buffer,
                pltpu.SemaphoreType.DMA((3,)),
                pltpu.SemaphoreType.DMA((2, PIECES)),
                pltpu.SemaphoreType.DMA((PIECES,)),
            ],
            10 * SLOTS * width * hidden,
            room=60,
        )
        return out

    at_b1 = plane(send_b1)
    a_one, x_two = gather_z(after(act_a[0], line[-1])), gather_z(after(act_b2[0], line[-1]))
    send_f1 = dispatch(0, a_one)
    send_x2 = dispatch(3, x_two)
    at_f1 = plane(after(send_f1, at_b1, send_x2))
    back_b1 = plane(after(backward(at_b1, at_b1, 1), at_f1))
    back_f1 = plane(after(forward(at_f1), back_b1))
    parts_b = combine(1, back_b1)
    grad_one, cot_two = onward(parts_b, section == 0, enter_grad, -1)
    at_x2 = plane(after(send_x2, back_f1, grad_one))
    parts_f = combine(0, back_f1)
    fwd_one, in_two = onward(parts_f, section == last, enter_a, 1)
    at_c2 = plane(after(dispatch(3, cot_two), at_x2))
    at_f2 = plane(after(dispatch(2, in_two), at_c2))
    back_b2 = plane(after(backward(at_x2, at_c2, 0), at_f2))
    back_f2 = plane(after(forward(at_f2), back_b2))
    grad_two = finish(combine(3, back_b2))
    fwd_two = finish(combine(2, back_f2))
    return fwd_one[None], grad_one[None], fwd_two[None], grad_two[None]


def solution(mesh):
    segments, experts = mesh.devices.shape
    grid = Mesh(
        mesh.devices.reshape(segments, NZ, SIDE, experts // NZ // SIDE),
        ("segment", "z", "x", "y"),
    )
    spread = ("z", "x", "y")
    tokens = P("segment", spread, None)
    weights = P("segment", spread, None, None)
    in_specs = (tokens,) * 12 + (P(spread, None),) * 2 + (weights,) * 3
    return jax.shard_map(
        shards, mesh=grid, in_specs=in_specs, out_specs=(tokens,) * 4, check_vma=False
    )
```

profile of v0, /device:TPU:8, one launch (start us, length us, event | category | flops | bytes accessed | tf_op | source)
XLA Modules:
  0.0 245.3 jit_solution(7363885194095510814)
XLA Ops:
  2.4 4.6 %collective-permute-start.2 = (bf16[24,4224]{1,0:T(8,128)(2,1)}, bf16[24,4224]{1,0:T(8,128)(2,1)S(1)}, u32[]{:S(2)}, u32[]{:S(2)}) collective-permute-start(bf16[24,4224]{1,0:T(8,128)(2,1)} %pack.1.m0.p0), channel_id=1, source_target_pairs={{0,48},{16,0},{32,16},{48,32},{1,49},{17,1},{33,17},{49,33},{2,50}... | collective-permute-start | bytes 608264 | tf_op jit(solution)/shard_map/ppermute | solution.py:307
  7.7 5.1 %collective-permute-done.2.m3.p3 = bf16[24,4224]{1,0:T(8,128)(2,1)S(1)} collective-permute-done((bf16[24,4224]{1,0:T(8,128)(2,1)}, bf16[24,4224]{1,0:T(8,128)(2,1)S(1)}, u32[]{:S(2)}, u32[]{:S(2)}) %collective-permute-start.2) | collective-permute-done | bytes 202784 | tf_op jit(solution)/shard_map/ppermute | solution.py:307
  12.8 11.1 %collective-permute-done.1.m2.p2 = bf16[24,4224]{1,0:T(8,128)(2,1)S(1)} collective-permute-done((bf16[24,4224]{1,0:T(8,128)(2,1)}, bf16[24,4224]{1,0:T(8,128)(2,1)S(1)}, u32[]{:S(2)}, u32[]{:S(2)}) %collective-permute-start.1) | collective-permute-done | bytes 202784 | tf_op jit(solution)/shard_map/ppermute | solution.py:307
  28.4 7.5 %all-to-all-start = ((bf16[16,16,4096]{2,1,0:T(8,128)(2,1)}), bf16[16,16,4096]{2,1,0:T(8,128)(2,1)}, u32[]{:S(2)}, u32[]{:S(2)}) async-start(bf16[16,16,4096]{2,1,0:T(8,128)(2,1)} %bitcast.22), calls=%async_computation | async-start | bytes 4194304 | tf_op jit(solution)/shard_map/all_to_all | solution.py:326
  47.1 7.4 %collective-permute-done.4.p2 = bf16[24,2048]{1,0:T(8,128)(2,1)S(1)} collective-permute-done((bf16[24,2048]{1,0:T(8,128)(2,1)S(1)}, bf16[24,2048]{1,0:T(8,128)(2,1)S(1)}, u32[]{:S(2)}, u32[]{:S(2)}) %collective-permute-start.4) | collective-permute-done | bytes 98336 | tf_op jit(solution)/shard_map/ppermute | solution.py:307
  58.4 5.9 %all-to-all-done = bf16[16,16,4096]{2,1,0:T(8,128)(2,1)} async-done(((bf16[16,16,4096]{2,1,0:T(8,128)(2,1)}), bf16[16,16,4096]{2,1,0:T(8,128)(2,1)}, u32[]{:S(2)}, u32[]{:S(2)}) %all-to-all-start) | async-done | bytes 2097184 | tf_op jit(solution)/shard_map/all_to_all | solution.py:326
  64.3 5.3 %all-to-all-start.1 = ((bf16[16,16,2048]{2,1,0:T(8,128)(2,1)}), bf16[16,16,2048]{2,1,0:T(8,128)(2,1)S(1)}, u32[]{:S(2)}, u32[]{:S(2)}) async-start(bf16[16,16,2048]{2,1,0:T(8,128)(2,1)} %bitcast.25), calls=%async_computation.1 | async-start | bytes 2097152 | tf_op jit(solution)/shard_map/all_to_all | solution.py:326
  69.6 10.9 %backward.2 = bf16[256,2048]{1,0:T(8,128)(2,1)} custom-call(bf16[256,4096]{1,0:T(8,128)(2,1)} %bitcast.23.xs.cs, bf16[256,4096]{1,0:T(8,128)(2,1)} %bitcast.23.xs.cs, bf16[2048,768]{1,0:T(8,128)(2,1)} %bitcast.69, bf16[2048,768]{1,0:T(8,128)(2,1)} %bitcast.73, bf16[768,2048]{1,0:T(8,128)(2,1)} %bitcast.77), custom_call_target="tpu_custom_call" | custom-call | flops 4026531840 | bytes 14680064 | tf_op jit(solution)/shard_map/backward/pallas_call | solution.py:288
  83.0 4.9 %all-to-all-start.2 = ((bf16[16,16,2048]{2,1,0:T(8,128)(2,1)}), bf16[16,16,2048]{2,1,0:T(8,128)(2,1)S(1)}, u32[]{:S(2)}, u32[]{:S(2)}) async-start(bf16[16,16,2048]{2,1,0:T(8,128)(2,1)} %bitcast.87), calls=%async_computation.2 | async-start | bytes 2097152 | tf_op jit(solution)/shard_map/all_to_all | solution.py:326
  87.9 8.8 %forward.2 = bf16[256,2048]{1,0:T(8,128)(2,1)} custom-call(bf16[256,2048]{1,0:T(8,128)(2,1)} %bitcast.84, bf16[2048,768]{1,0:T(8,128)(2,1)} %bitcast.70, bf16[2048,768]{1,0:T(8,128)(2,1)} %bitcast.74, bf16[768,2048]{1,0:T(8,128)(2,1)} %bitcast.78), custom_call_target="tpu_custom_call" | custom-call | flops 2415919104 | bytes 11534336 | tf_op jit(solution)/shard_map/forward/pallas_call | solution.py:288
  96.7 5.2 %all-to-all-done.2 = bf16[16,16,2048]{2,1,0:T(8,128)(2,1)S(1)} async-done(((bf16[16,16,2048]{2,1,0:T(8,128)(2,1)}), bf16[16,16,2048]{2,1,0:T(8,128)(2,1)S(1)}, u32[]{:S(2)}, u32[]{:S(2)}) %all-to-all-start.2) | async-done | bytes 1048608 | tf_op jit(solution)/shard_map/all_to_all | solution.py:326
  101.9 5.0 %all-to-all-start.3 = ((bf16[16,16,2048]{2,1,0:T(8,128)(2,1)}), bf16[16,16,2048]{2,1,0:T(8,128)(2,1)S(1)}, u32[]{:S(2)}, u32[]{:S(2)}) async-start(bf16[16,16,2048]{2,1,0:T(8,128)(2,1)} %bitcast.81), calls=%async_computation.3 | async-start | bytes 2097152 | tf_op jit(solution)/shard_map/all_to_all | solution.py:326
  121.5 5.5 %all-to-all-start.4 = ((bf16[16,16,2048]{2,1,0:T(8,128)(2,1)}), bf16[16,16,2048]{2,1,0:T(8,128)(2,1)}, u32[]{:S(2)}, u32[]{:S(2)}) async-start(bf16[16,16,2048]{2,1,0:T(8,128)(2,1)} %bitcast.60), calls=%async_computation.4 | async-start | bytes 2097152 | tf_op jit(solution)/shard_map/all_to_all | solution.py:326
  141.8 6.0 %collective-permute-done.16.p1 = bf16[24,2048]{1,0:T(8,128)(2,1)S(1)} collective-permute-done((bf16[24,2048]{1,0:T(8,128)(2,1)S(1)}, bf16[24,2048]{1,0:T(8,128)(2,1)S(1)}, u32[]{:S(2)}, u32[]{:S(2)}) %collective-permute-start.16) | collective-permute-done | bytes 98336 | tf_op jit(solution)/shard_map/ppermute | solution.py:317
  149.3 7.3 %all-to-all-start.5 = ((bf16[16,16,2048]{2,1,0:T(8,128)(2,1)}), bf16[16,16,2048]{2,1,0:T(8,128)(2,1)S(1)}, u32[]{:S(2)}, u32[]{:S(2)}) async-start(bf16[16,16,2048]{2,1,0:T(8,128)(2,1)} %bitcast.38), calls=%async_computation.5 | async-start | bytes 2097152 | tf_op jit(solution)/shard_map/all_to_all | solution.py:326
  160.8 5.8 %collective-permute-done.22.p3 = bf16[24,2048]{1,0:T(8,128)(2,1)S(1)} collective-permute-done((bf16[24,2048]{1,0:T(8,128)(2,1)S(1)}, bf16[24,2048]{1,0:T(8,128)(2,1)S(1)}, u32[]{:S(2)}, u32[]{:S(2)}) %collective-permute-start.22) | collective-permute-done | bytes 98336 | tf_op jit(solution)/shard_map/ppermute | solution.py:317
  173.0 7.2 %all-to-all-start.6 = ((bf16[16,16,2048]{2,1,0:T(8,128)(2,1)}), bf16[16,16,2048]{2,1,0:T(8,128)(2,1)S(1)}, u32[]{:S(2)}, u32[]{:S(2)}) async-start(bf16[16,16,2048]{2,1,0:T(8,128)(2,1)} %bitcast.40), calls=%async_computation.6 | async-start | bytes 2097152 | tf_op jit(solution)/shard_map/all_to_all | solution.py:326
  180.2 10.8 %backward.3 = bf16[256,2048]{1,0:T(8,128)(2,1)} custom-call(bf16[256,2048]{1,0:T(8,128)(2,1)} %bitcast.37.xs, bf16[256,2048]{1,0:T(8,128)(2,1)} %bitcast.85, bf16[2048,768]{1,0:T(8,128)(2,1)} %bitcast.71, bf16[2048,768]{1,0:T(8,128)(2,1)} %bitcast.75, bf16[768,2048]{1,0:T(8,128)(2,1)} %bitcast.79), custom_call_target="tpu_custom_call" | custom-call | flops 4026531840 | bytes 12582912 | tf_op jit(solution)/shard_map/backward/pallas_call | solution.py:288
  191.0 5.8 %all-to-all-done.6 = bf16[16,16,2048]{2,1,0:T(8,128)(2,1)S(1)} async-done(((bf16[16,16,2048]{2,1,0:T(8,128)(2,1)}), bf16[16,16,2048]{2,1,0:T(8,128)(2,1)S(1)}, u32[]{:S(2)}, u32[]{:S(2)}) %all-to-all-start.6) | async-done | bytes 1048608 | tf_op jit(solution)/shard_map/all_to_all | solution.py:326
  196.8 4.9 %all-to-all-start.7 = ((bf16[16,16,2048]{2,1,0:T(8,128)(2,1)}), bf16[16,16,2048]{2,1,0:T(8,128)(2,1)S(1)}, u32[]{:S(2)}, u32[]{:S(2)}) async-start(bf16[16,16,2048]{2,1,0:T(8,128)(2,1)} %bitcast.86), calls=%async_computation.7 | async-start | bytes 2097152 | tf_op jit(solution)/shard_map/all_to_all | solution.py:326
  201.7 8.8 %forward.3 = bf16[256,2048]{1,0:T(8,128)(2,1)} custom-call(bf16[256,2048]{1,0:T(8,128)(2,1)} %bitcast.83, bf16[2048,768]{1,0:T(8,128)(2,1)} %bitcast.72, bf16[2048,768]{1,0:T(8,128)(2,1)} %bitcast.76, bf16[768,2048]{1,0:T(8,128)(2,1)} %bitcast.80), custom_call_target="tpu_custom_call" | custom-call | flops 2415919104 | bytes 11534336 | tf_op jit(solution)/shard_map/forward/pallas_call | solution.py:288
  210.5 5.6 %all-to-all-done.7 = bf16[16,16,2048]{2,1,0:T(8,128)(2,1)S(1)} async-done(((bf16[16,16,2048]{2,1,0:T(8,128)(2,1)}), bf16[16,16,2048]{2,1,0:T(8,128)(2,1)S(1)}, u32[]{:S(2)}, u32[]{:S(2)}) %all-to-all-start.7) | async-done | bytes 1048608 | tf_op jit(solution)/shard_map/all_to_all | solution.py:326
  216.1 4.9 %all-to-all-start.8 = ((bf16[16,16,2048]{2,1,0:T(8,128)(2,1)}), bf16[16,16,2048]{2,1,0:T(8,128)(2,1)S(1)}, u32[]{:S(2)}, u32[]{:S(2)}) async-start(bf16[16,16,2048]{2,1,0:T(8,128)(2,1)} %bitcast.82), calls=%async_computation.8 | async-start | bytes 2097152 | tf_op jit(solution)/shard_map/all_to_all | solution.py:326
  238.4 4.7 %collective-permute-done.26.b1 = bf16[24,2048]{1,0:T(8,128)(2,1)S(1)} collective-permute-done((bf16[24,2048]{1,0:T(8,128)(2,1)S(1)}, bf16[24,2048]{1,0:T(8,128)(2,1)S(1)}, u32[]{:S(2)}, u32[]{:S(2)}) %collective-permute-start.26) | collective-permute-done | bytes 98336 | tf_op jit(solution)/shard_map/ppermute | solution.py:307
  (91 shorter events, 85.5 us)
Async XLA Ops:
  2.4 10.4 %collective-permute-start.2 = (bf16[24,4224]{1,0:T(8,128)(2,1)}, bf16[24,4224]{1,0:T(8,128)(2,1)S(1)}, u32[]{:S(2)}, u32[]{:S(2)}) collective-permute-start(bf16[24,4224]{1,0:T(8,128)(2,1)} %pack.1.m0.p0), channel_id=1, source_target_pairs={{0,48},{16,0},{32,16},{48,32},{1,49},{17,1},{33,17},{49,33},{2,50}... | collective-permute-start | bytes 608264 | tf_op jit(solution)/shard_map/ppermute | solution.py:307
  7.0 16.9 %collective-permute-start.1 = (bf16[24,4224]{1,0:T(8,128)(2,1)}, bf16[24,4224]{1,0:T(8,128)(2,1)S(1)}, u32[]{:S(2)}, u32[]{:S(2)}) collective-permute-start(bf16[24,4224]{1,0:T(8,128)(2,1)} %pack.1.m0.p0), channel_id=1, source_target_pairs={{0,32},{16,48},{32,0},{48,16},{1,33},{17,49},{33,1},{49,17},{2,34}... | collective-permute-start | bytes 608264 | tf_op jit(solution)/shard_map/ppermute | solution.py:307
  7.0 16.9 %collective-permute-start = (bf16[24,4224]{1,0:T(8,128)(2,1)}, bf16[24,4224]{1,0:T(8,128)(2,1)S(1)}, u32[]{:S(2)}, u32[]{:S(2)}) collective-permute-start(bf16[24,4224]{1,0:T(8,128)(2,1)} %pack.1.m0.p0), channel_id=1, source_target_pairs={{0,16},{16,32},{32,48},{48,0},{1,17},{17,33},{33,49},{49,1},{2,18}... | collective-permute-start | bytes 608264 | tf_op jit(solution)/shard_map/ppermute | solution.py:307
  28.4 35.9 %all-to-all-start = ((bf16[16,16,4096]{2,1,0:T(8,128)(2,1)}), bf16[16,16,4096]{2,1,0:T(8,128)(2,1)}, u32[]{:S(2)}, u32[]{:S(2)}) async-start(bf16[16,16,4096]{2,1,0:T(8,128)(2,1)} %bitcast.22), calls=%async_computation | async-start | bytes 4194304 | tf_op jit(solution)/shard_map/all_to_all | solution.py:326
  38.0 16.4 %collective-permute-start.4 = (bf16[24,2048]{1,0:T(8,128)(2,1)S(1)}, bf16[24,2048]{1,0:T(8,128)(2,1)S(1)}, u32[]{:S(2)}, u32[]{:S(2)}) collective-permute-start(bf16[24,2048]{1,0:T(8,128)(2,1)S(1)} %bitcast.62), channel_id=1, source_target_pairs={{0,32},{16,48},{32,0},{48,16},{1,33},{17,49},{33,1},{49,17},{2,34}... | collective-permute-start | bytes 294920 | tf_op jit(solution)/shard_map/ppermute | solution.py:307
  40.5 13.9 %collective-permute-start.3 = (bf16[24,2048]{1,0:T(8,128)(2,1)S(1)}, bf16[24,2048]{1,0:T(8,128)(2,1)S(1)}, u32[]{:S(2)}, u32[]{:S(2)}) collective-permute-start(bf16[24,2048]{1,0:T(8,128)(2,1)S(1)} %bitcast.63), channel_id=1, source_target_pairs={{0,16},{16,32},{32,48},{48,0},{1,17},{17,33},{33,49},{49,1},{2,18}... | collective-permute-start | bytes 294920 | tf_op jit(solution)/shard_map/ppermute | solution.py:307
  42.4 13.4 %collective-permute-start.8 = (bf16[24,2048]{1,0:T(8,128)(2,1)S(1)}, bf16[24,2048]{1,0:T(8,128)(2,1)S(1)}, u32[]{:S(2)}, u32[]{:S(2)}) collective-permute-start(bf16[24,2048]{1,0:T(8,128)(2,1)S(1)} %bitcast.65), channel_id=1, source_target_pairs={{0,48},{16,0},{32,16},{48,32},{1,49},{17,1},{33,17},{49,33},{2,50}... | collective-permute-start | bytes 294920 | tf_op jit(solution)/shard_map/ppermute | solution.py:307
  44.3 12.4 %collective-permute-start.7 = (bf16[24,2048]{1,0:T(8,128)(2,1)S(1)}, bf16[24,2048]{1,0:T(8,128)(2,1)S(1)}, u32[]{:S(2)}, u32[]{:S(2)}) collective-permute-start(bf16[24,2048]{1,0:T(8,128)(2,1)S(1)} %bitcast.66), channel_id=1, source_target_pairs={{0,32},{16,48},{32,0},{48,16},{1,33},{17,49},{33,1},{49,17},{2,34}... | collective-permute-start | bytes 294920 | tf_op jit(solution)/shard_map/ppermute | solution.py:307
  44.4 12.4 %collective-permute-start.6 = (bf16[24,2048]{1,0:T(8,128)(2,1)S(1)}, bf16[24,2048]{1,0:T(8,128)(2,1)S(1)}, u32[]{:S(2)}, u32[]{:S(2)}) collective-permute-start(bf16[24,2048]{1,0:T(8,128)(2,1)S(1)} %bitcast.67), channel_id=1, source_target_pairs={{0,16},{16,32},{32,48},{48,0},{1,17},{17,33},{33,49},{49,1},{2,18}... | collective-permute-start | bytes 294920 | tf_op jit(solution)/shard_map/ppermute | solution.py:307
  64.3 18.7 %all-to-all-start.1 = ((bf16[16,16,2048]{2,1,0:T(8,128)(2,1)}), bf16[16,16,2048]{2,1,0:T(8,128)(2,1)S(1)}, u32[]{:S(2)}, u32[]{:S(2)}) async-start(bf16[16,16,2048]{2,1,0:T(8,128)(2,1)} %bitcast.25), calls=%async_computation.1 | async-start | bytes 2097152 | tf_op jit(solution)/shard_map/all_to_all | solution.py:326
  83.0 18.9 %all-to-all-start.2 = ((bf16[16,16,2048]{2,1,0:T(8,128)(2,1)}), bf16[16,16,2048]{2,1,0:T(8,128)(2,1)S(1)}, u32[]{:S(2)}, u32[]{:S(2)}) async-start(bf16[16,16,2048]{2,1,0:T(8,128)(2,1)} %bitcast.87), calls=%async_computation.2 | async-start | bytes 2097152 | tf_op jit(solution)/shard_map/all_to_all | solution.py:326
  101.9 19.6 %all-to-all-start.3 = ((bf16[16,16,2048]{2,1,0:T(8,128)(2,1)}), bf16[16,16,2048]{2,1,0:T(8,128)(2,1)S(1)}, u32[]{:S(2)}, u32[]{:S(2)}) async-start(bf16[16,16,2048]{2,1,0:T(8,128)(2,1)} %bitcast.81), calls=%async_computation.3 | async-start | bytes 2097152 | tf_op jit(solution)/shard_map/all_to_all | solution.py:326
  121.5 27.8 %all-to-all-start.4 = ((bf16[16,16,2048]{2,1,0:T(8,128)(2,1)}), bf16[16,16,2048]{2,1,0:T(8,128)(2,1)}, u32[]{:S(2)}, u32[]{:S(2)}) async-start(bf16[16,16,2048]{2,1,0:T(8,128)(2,1)} %bitcast.60), calls=%async_computation.4 | async-start | bytes 2097152 | tf_op jit(solution)/shard_map/all_to_all | solution.py:326
  127.9 10.1 %collective-permute-start.12 = (bf16[24,2048]{1,0:T(8,128)(2,1)S(1)}, bf16[24,2048]{1,0:T(8,128)(2,1)S(1)}, u32[]{:S(2)}, u32[]{:S(2)}) collective-permute-start(bf16[24,2048]{1,0:T(8,128)(2,1)S(1)} %get-tuple-element.75), channel_id=1, source_target_pairs={{0,48},{16,0},{32,16},{48,32},{1,49},{17,1},{33,17},{49,33},{2,50}... | collective-permute-start | bytes 294920 | tf_op jit(solution)/shard_map/ppermute | solution.py:307
  128.3 11.6 %collective-permute-start.13 = (bf16[24,2048]{1,0:T(8,128)(2,1)S(1)}, bf16[24,2048]{1,0:T(8,128)(2,1)S(1)}, u32[]{:S(2)}, u32[]{:S(2)}) collective-permute-start(bf16[24,2048]{1,0:T(8,128)(2,1)S(1)} %get-tuple-element.76), channel_id=1, source_target_pairs={{0,32},{16,48},{32,0},{48,16},{1,33},{17,49},{33,1},{49,17},{2,34}... | collective-permute-start | bytes 294920 | tf_op jit(solution)/shard_map/ppermute | solution.py:307
  130.0 11.1 %collective-permute-start.14 = (bf16[24,2048]{1,0:T(8,128)(2,1)S(1)}, bf16[24,2048]{1,0:T(8,128)(2,1)S(1)}, u32[]{:S(2)}, u32[]{:S(2)}) collective-permute-start(bf16[24,2048]{1,0:T(8,128)(2,1)S(1)} %get-tuple-element.77), channel_id=1, source_target_pairs={{0,16},{16,32},{32,48},{48,0},{1,17},{17,33},{33,49},{49,1},{2,18}... | collective-permute-start | bytes 294920 | tf_op jit(solution)/shard_map/ppermute | solution.py:307
  131.9 9.9 %collective-permute-start.18 = (bf16[24,2048]{1,0:T(8,128)(2,1)S(1)}, bf16[24,2048]{1,0:T(8,128)(2,1)S(1)}, u32[]{:S(2)}, u32[]{:S(2)}) collective-permute-start(bf16[24,2048]{1,0:T(8,128)(2,1)S(1)} %get-tuple-element.80), channel_id=1, source_target_pairs={{0,240},{16,192},{32,208},{48,224},{64,48},{80,0},{96,16},{112,32}... | collective-permute-start | bytes 294920 | tf_op jit(solution)/shard_map/ppermute | solution.py:317
  138.0 9.8 %collective-permute-start.16 = (bf16[24,2048]{1,0:T(8,128)(2,1)S(1)}, bf16[24,2048]{1,0:T(8,128)(2,1)S(1)}, u32[]{:S(2)}, u32[]{:S(2)}) collective-permute-start(bf16[24,2048]{1,0:T(8,128)(2,1)S(1)} %get-tuple-element.80), channel_id=1, source_target_pairs={{0,208},{16,224},{32,240},{48,192},{64,16},{80,32},{96,48},{112,0}... | collective-permute-start | bytes 294920 | tf_op jit(solution)/shard_map/ppermute | solution.py:317
  149.3 22.7 %all-to-all-start.5 = ((bf16[16,16,2048]{2,1,0:T(8,128)(2,1)}), bf16[16,16,2048]{2,1,0:T(8,128)(2,1)S(1)}, u32[]{:S(2)}, u32[]{:S(2)}) async-start(bf16[16,16,2048]{2,1,0:T(8,128)(2,1)} %bitcast.38), calls=%async_computation.5 | async-start | bytes 2097152 | tf_op jit(solution)/shard_map/all_to_all | solution.py:326
  156.6 10.0 %collective-permute-start.22 = (bf16[24,2048]{1,0:T(8,128)(2,1)S(1)}, bf16[24,2048]{1,0:T(8,128)(2,1)S(1)}, u32[]{:S(2)}, u32[]{:S(2)}) collective-permute-start(bf16[24,2048]{1,0:T(8,128)(2,1)S(1)} %get-tuple-element.82), channel_id=1, source_target_pairs={{0,112},{16,64},{32,80},{48,96},{64,176},{80,128},{96,144},{112,16... | collective-permute-start | bytes 294920 | tf_op jit(solution)/shard_map/ppermute | solution.py:317
  160.6 9.9 %collective-permute-start.19 = (bf16[24,2048]{1,0:T(8,128)(2,1)S(1)}, bf16[24,2048]{1,0:T(8,128)(2,1)S(1)}, u32[]{:S(2)}, u32[]{:S(2)}) collective-permute-start(bf16[24,2048]{1,0:T(8,128)(2,1)S(1)} %get-tuple-element.82), channel_id=1, source_target_pairs={{0,64},{16,80},{32,96},{48,112},{64,128},{80,144},{96,160},{112,17... | collective-permute-start | bytes 294920 | tf_op jit(solution)/shard_map/ppermute | solution.py:317
  173.0 23.8 %all-to-all-start.6 = ((bf16[16,16,2048]{2,1,0:T(8,128)(2,1)}), bf16[16,16,2048]{2,1,0:T(8,128)(2,1)S(1)}, u32[]{:S(2)}, u32[]{:S(2)}) async-start(bf16[16,16,2048]{2,1,0:T(8,128)(2,1)} %bitcast.40), calls=%async_computation.6 | async-start | bytes 2097152 | tf_op jit(solution)/shard_map/all_to_all | solution.py:326
  196.8 19.3 %all-to-all-start.7 = ((bf16[16,16,2048]{2,1,0:T(8,128)(2,1)}), bf16[16,16,2048]{2,1,0:T(8,128)(2,1)S(1)}, u32[]{:S(2)}, u32[]{:S(2)}) async-start(bf16[16,16,2048]{2,1,0:T(8,128)(2,1)} %bitcast.86), calls=%async_computation.7 | async-start | bytes 2097152 | tf_op jit(solution)/shard_map/all_to_all | solution.py:326
  216.1 19.3 %all-to-all-start.8 = ((bf16[16,16,2048]{2,1,0:T(8,128)(2,1)}), bf16[16,16,2048]{2,1,0:T(8,128)(2,1)S(1)}, u32[]{:S(2)}, u32[]{:S(2)}) async-start(bf16[16,16,2048]{2,1,0:T(8,128)(2,1)} %bitcast.82), calls=%async_computation.8 | async-start | bytes 2097152 | tf_op jit(solution)/shard_map/all_to_all | solution.py:326
  (24 other events, 210.1 us)
where the time goes:
time: 246 us; the launch traced here: 245 us
  starting transfers between devices  93.3 us (38%)
  waiting for transfers between devices  90.3 us (37%)
  Pallas kernels  57.9 us (24%)
  local copies, waits for them, and re-layouts  2.94 us (1%)
    pallas_call x19, Pallas kernels, call(): pl.pallas_call(kernel, name=name, grid=grid, in_specs=in_specs, out_specs...  57.9 us
    all_to_all x9, starting transfers between devices, plane(): lax.all_to_all(block, ('x', 'y'), split_axis=0, concat_axis=0, tiled=True)  52.5 us
    ppermute x21, waiting for transfers between devices, shift(): return lax.ppermute(block, axis, [(i, (i + k) % size) for i in range(size)])  42.9 us
    all_to_all x9, waiting for transfers between devices, plane(): lax.all_to_all(block, ('x', 'y'), split_axis=0, concat_axis=0, tiled=True)  31.7 us
    ppermute x21, starting transfers between devices, shift(): return lax.ppermute(block, axis, [(i, (i + k) % size) for i in range(size)])  27.4 us
    ppermute x8, waiting for transfers between devices, to_section(): return lax.ppermute(block, ('segment', 'z'), route)  15.7 us
    ppermute x8, starting transfers between devices, to_section(): return lax.ppermute(block, ('segment', 'z'), route)  13.4 us
  transfers between devices with their start and end apart: 38, of which 21 were waited for; matrix products, arithmetic and copies ran while one was open for 0% of the time, Pallas kernels for 21%

commit v1 on v0

--- a/solution.py
+++ b/solution.py
@@ -199,31 +199,43 @@
 
 def forward_kernel(rows, w_gate, w_up, w_down, result, *scratch):
     x, gate_mat, up_mat, down_mat, out, gate_pre, up_pre, hidden, sems, semp, sent = scratch
-    whole = ((rows, x), (w_down, down_mat))
     gate, up = (w_gate, gate_mat), (w_up, up_mat)
-    begin(whole[:1], (gate, up), sems, semp)
+    begin(((rows, x),), (gate, up), sems, semp)
     pltpu.make_async_copy(w_down, down_mat, sems.at[1]).start()
     pltpu.make_async_copy(rows, x, sems.at[0]).wait()
     pre_activations(x, gate, up, semp, gate_pre, up_pre)
     hidden[...] = (jax.nn.silu(gate_pre[...]) * up_pre[...]).astype(BF16)
     pltpu.make_async_copy(w_down, down_mat, sems.at[1]).wait()
+    target = result.at[:, pl.ds(0, out.shape[1])]
 
     def step(k):
         column(out, k)[...] = dot(hidden[...], column(down_mat, k)[...]).astype(BF16)
-        send(out, result, sent, k).start()
+        send(out, target, sent, k).start()
 
     loop(step)
     for k in range(PIECES):
-        send(out, result, sent, k).wait()
-
-
-def backward_kernel(place, xs, cs, w_gate, w_up, w_down, result, *scratch):
+        send(out, target, sent, k).wait()
+
+
+def joined_kernel(rows, w_gate, w_up, w_down, extra, result, *scratch):
+    held, sem = scratch[-2:]
+    width = extra.shape[1]
+    into = pltpu.make_async_copy(extra, held, sem.at[0])
+    onto = pltpu.make_async_copy(held, result.at[:, pl.ds(width, width)], sem.at[1])
+    into.start()
+    into.wait()
+    onto.start()
+    forward_kernel(rows, w_gate, w_up, w_down, result, *scratch[:-2])
+    onto.wait()
+
+
+def backward_kernel(first, second, xs, cs, w_gate, w_up, w_down, result, *scratch):
     x, c, gate_mat, up_mat, down_mat, out = scratch[:6]
     gate_pre, up_pre, d_gate, d_upper, sems, semp, sent = scratch[6:]
     width = x.shape[1]
     gate, up = (w_gate, gate_mat), (w_up, up_mat)
-    rows = pltpu.make_async_copy(xs.at[:, pl.ds(0, width)], x, sems.at[0])
-    cots = pltpu.make_async_copy(cs.at[:, pl.ds(place * width, width)], c, sems.at[1])
+    rows = pltpu.make_async_copy(xs.at[:, pl.ds(first * width, width)], x, sems.at[0])
+    cots = pltpu.make_async_copy(cs.at[:, pl.ds(second * width, width)], c, sems.at[1])
     downs = pltpu.make_async_copy(w_down, down_mat, sems.at[2])
     rows.start()
     begin((), (gate, up), sems, semp)
@@ -451,15 +463,15 @@
     thin_buffer = pltpu.VMEM((SLOTS, hidden), BF16)
     mat_buffers = [pltpu.VMEM(m.shape, BF16) for m in mats]
 
-    def forward(rows):
+    def forward(rows, *extra):
         (out,) = run(
-            forward_kernel,
+            joined_kernel if extra else forward_kernel,
             "forward",
             (),
-            [ANY] + [HBM] * 3,
-            (rows,) + mats,
+            [ANY] + [HBM] * 3 + [ANY] * len(extra),
+            (rows,) + mats + extra,
             [ANY],
-            [buffer],
+            [shaped(SLOTS, width * (1 + len(extra)))],
             [rows_buffer]
             + mat_buffers
             + [
@@ -470,15 +482,16 @@
                 pltpu.SemaphoreType.DMA((2,)),
                 pltpu.SemaphoreType.DMA((2, PIECES)),
                 pltpu.SemaphoreType.DMA((PIECES,)),
-            ],
+            ]
+            + [rows_buffer, pltpu.SemaphoreType.DMA((2,))] * len(extra),
             6 * SLOTS * width * hidden,
             room=60,
         )
         return out
 
-    def backward(x, c, column):
+    def backward(x, c, first, second):
         (out,) = run(
-            functools.partial(backward_kernel, column),
+            functools.partial(backward_kernel, first, second),
             "backward",
             (),
             [ANY] * 2 + [HBM] * 3,
@@ -507,16 +520,16 @@
     send_f1 = dispatch(0, a_one)
     send_x2 = dispatch(3, x_two)
     at_f1 = plane(after(send_f1, at_b1, send_x2))
-    back_b1 = plane(after(backward(at_b1, at_b1, 1), at_f1))
-    back_f1 = plane(after(forward(at_f1), back_b1))
+    back_b1 = plane(after(backward(at_b1, at_b1, 0, 1), at_f1))
+    back_f1 = plane(after(forward(at_f1, send_x2), back_b1))
     parts_b = combine(1, back_b1)
     grad_one, cot_two = onward(parts_b, section == 0, enter_grad, -1)
-    at_x2 = plane(after(send_x2, back_f1, grad_one))
+    send_c2 = dispatch(3, cot_two)
+    at_c2 = plane(after(send_c2, back_f1))
     parts_f = combine(0, back_f1)
     fwd_one, in_two = onward(parts_f, section == last, enter_a, 1)
-    at_c2 = plane(after(dispatch(3, cot_two), at_x2))
     at_f2 = plane(after(dispatch(2, in_two), at_c2))
-    back_b2 = plane(after(backward(at_x2, at_c2, 0), at_f2))
+    back_b2 = plane(after(backward(back_f1, at_c2, 1, 0), at_f2))
     back_f2 = plane(after(forward(at_f2), back_b2))
     grad_two = finish(combine(3, back_b2))
     fwd_two = finish(combine(2, back_f2))

time: 246 us -> 245 us (level)
  waiting for transfers between devices: 90.3 us -> 84.9 us
    all_to_all x9 -> x8, waiting for transfers between devices: 31.7 us -> 22.3 us  [plane(): lax.all_to_all(block, ('x', 'y'), split_axis=0, concat_axis=0, tiled=True)]
    ppermute x21, waiting for transfers between devices: 42.9 us -> 48.7 us  [shift(): return lax.ppermute(block, axis, [(i, (i + k) % size) for i in range(size)])]
    all_to_all x9 -> x8, starting transfers between devices: 52.5 us -> 47.5 us  [plane(): lax.all_to_all(block, ('x', 'y'), split_axis=0, concat_axis=0, tiled=True)]
    unnamed x20 -> x26, local copies, waits for them, and re-layouts: 2.94 us -> 5.13 us
  transfers between devices with their start and end apart: 38 -> 37, of which waited for: 21 -> 23; matrix products, arithmetic and copies ran while one was open for 0% -> 0% of each run, Pallas kernels for 21% -> 22%
where the time goes in v1:
time: 245 us; the launch traced here: 244 us
  starting transfers between devices  92.7 us (38%)
  waiting for transfers between devices  84.9 us (35%)
  Pallas kernels  60.2 us (25%)
  local copies, waits for them, and re-layouts  5.13 us (2%)
    pallas_call x19, Pallas kernels, call(): pl.pallas_call(kernel, name=name, grid=grid, in_specs=in_specs, out_specs...  60.2 us
    ppermute x21, waiting for transfers between devices, shift(): return lax.ppermute(block, axis, [(i, (i + k) % size) for i in range(size)])  48.7 us
    all_to_all x8, starting transfers between devices, plane(): lax.all_to_all(block, ('x', 'y'), split_axis=0, concat_axis=0, tiled=True)  47.5 us
    ppermute x21, starting transfers between devices, shift(): return lax.ppermute(block, axis, [(i, (i + k) % size) for i in range(size)])  29.5 us
    all_to_all x8, waiting for transfers between devices, plane(): lax.all_to_all(block, ('x', 'y'), split_axis=0, concat_axis=0, tiled=True)  22.3 us
    ppermute x8, starting transfers between devices, to_section(): return lax.ppermute(block, ('segment', 'z'), route)  15.7 us
    ppermute x8, waiting for transfers between devices, to_section(): return lax.ppermute(block, ('segment', 'z'), route)  13.9 us
    unnamed x26, local copies, waits for them, and re-layouts  5.13 us
  transfers between devices with their start and end apart: 37, of which 23 were waited for; matrix products, arithmetic and copies ran while one was open for 0% of the time, Pallas kernels for 22%

profile of v1, /device:TPU:8, one launch (start us, length us, event | category | flops | bytes accessed | tf_op | source)
XLA Modules:
  0.0 243.7 jit_solution(15820096747257349168)
XLA Ops:
  2.4 4.6 %collective-permute-start.2 = (bf16[24,4224]{1,0:T(8,128)(2,1)}, bf16[24,4224]{1,0:T(8,128)(2,1)S(1)}, u32[]{:S(2)}, u32[]{:S(2)}) collective-permute-start(bf16[24,4224]{1,0:T(8,128)(2,1)} %pack.1.m0.p0), channel_id=1, source_target_pairs={{0,48},{16,0},{32,16},{48,32},{1,49},{17,1},{33,17},{49,33},{2,50}... | collective-permute-start | bytes 608264 | tf_op jit(solution)/shard_map/ppermute | solution.py:319
  7.7 5.1 %collective-permute-done.2.m3.p3 = bf16[24,4224]{1,0:T(8,128)(2,1)S(1)} collective-permute-done((bf16[24,4224]{1,0:T(8,128)(2,1)}, bf16[24,4224]{1,0:T(8,128)(2,1)S(1)}, u32[]{:S(2)}, u32[]{:S(2)}) %collective-permute-start.2) | collective-permute-done | bytes 202784 | tf_op jit(solution)/shard_map/ppermute | solution.py:319
  12.8 11.1 %collective-permute-done.1.m2.p2 = bf16[24,4224]{1,0:T(8,128)(2,1)S(1)} collective-permute-done((bf16[24,4224]{1,0:T(8,128)(2,1)}, bf16[24,4224]{1,0:T(8,128)(2,1)S(1)}, u32[]{:S(2)}, u32[]{:S(2)}) %collective-permute-start.1) | collective-permute-done | bytes 202784 | tf_op jit(solution)/shard_map/ppermute | solution.py:319
  28.4 7.5 %all-to-all-start = ((bf16[16,16,4096]{2,1,0:T(8,128)(2,1)}), bf16[16,16,4096]{2,1,0:T(8,128)(2,1)}, u32[]{:S(2)}, u32[]{:S(2)}) async-start(bf16[16,16,4096]{2,1,0:T(8,128)(2,1)} %bitcast.22), calls=%async_computation | async-start | bytes 4194304 | tf_op jit(solution)/shard_map/all_to_all | solution.py:338
  47.0 7.4 %collective-permute-done.4.p2 = bf16[24,2048]{1,0:T(8,128)(2,1)S(1)} collective-permute-done((bf16[24,2048]{1,0:T(8,128)(2,1)S(1)}, bf16[24,2048]{1,0:T(8,128)(2,1)S(1)}, u32[]{:S(2)}, u32[]{:S(2)}) %collective-permute-start.4) | collective-permute-done | bytes 98336 | tf_op jit(solution)/shard_map/ppermute | solution.py:319
  58.4 5.9 %all-to-all-done = bf16[16,16,4096]{2,1,0:T(8,128)(2,1)} async-done(((bf16[16,16,4096]{2,1,0:T(8,128)(2,1)}), bf16[16,16,4096]{2,1,0:T(8,128)(2,1)}, u32[]{:S(2)}, u32[]{:S(2)}) %all-to-all-start) | async-done | bytes 2097184 | tf_op jit(solution)/shard_map/all_to_all | solution.py:338
  64.3 5.3 %all-to-all-start.1 = ((bf16[16,16,2048]{2,1,0:T(8,128)(2,1)}), bf16[16,16,2048]{2,1,0:T(8,128)(2,1)S(1)}, u32[]{:S(2)}, u32[]{:S(2)}) async-start(bf16[16,16,2048]{2,1,0:T(8,128)(2,1)} %bitcast.25), calls=%async_computation.1 | async-start | bytes 2097152 | tf_op jit(solution)/shard_map/all_to_all | solution.py:338
  69.6 10.9 %backward.2 = bf16[256,2048]{1,0:T(8,128)(2,1)} custom-call(bf16[256,4096]{1,0:T(8,128)(2,1)} %bitcast.23.xs.cs, bf16[256,4096]{1,0:T(8,128)(2,1)} %bitcast.23.xs.cs, bf16[2048,768]{1,0:T(8,128)(2,1)} %bitcast.68, bf16[2048,768]{1,0:T(8,128)(2,1)} %bitcast.72, bf16[768,2048]{1,0:T(8,128)(2,1)} %bitcast.76), custom_call_target="tpu_custom_call" | custom-call | flops 4026531840 | bytes 14680064 | tf_op jit(solution)/shard_map/backward/pallas_call | solution.py:300
  83.0 4.9 %all-to-all-start.2 = ((bf16[16,16,2048]{2,1,0:T(8,128)(2,1)}), bf16[16,16,2048]{2,1,0:T(8,128)(2,1)S(1)}, u32[]{:S(2)}, u32[]{:S(2)}) async-start(bf16[16,16,2048]{2,1,0:T(8,128)(2,1)} %bitcast.84), calls=%async_computation.2 | async-start | bytes 2097152 | tf_op jit(solution)/shard_map/all_to_all | solution.py:338
  87.9 10.4 %forward.2 = bf16[256,4096]{1,0:T(8,128)(2,1)} custom-call(bf16[256,2048]{1,0:T(8,128)(2,1)} %bitcast.82, bf16[2048,768]{1,0:T(8,128)(2,1)} %bitcast.69, bf16[2048,768]{1,0:T(8,128)(2,1)} %bitcast.73, bf16[768,2048]{1,0:T(8,128)(2,1)} %bitcast.77, bf16[256,2048]{1,0:T(8,128)(2,1)} %copy-done.4), custom_call_target="tpu_custom_call" | custom-call | flops 2415919104 | bytes 13631488 | tf_op jit(solution)/shard_map/forward/pallas_call | solution.py:300
  102.9 5.1 %all-to-all-start.3 = ((bf16[16,16,4096]{2,1,0:T(8,128)(2,1)}), bf16[16,16,4096]{2,1,0:T(8,128)(2,1)S(1)}, u32[]{:S(2)}, u32[]{:S(2)}) async-start(bf16[16,16,4096]{2,1,0:T(8,128)(2,1)} %bitcast.80), calls=%async_computation.3 | async-start | bytes 4194304 | tf_op jit(solution)/shard_map/all_to_all | solution.py:338
  116.6 3.9 %collective-permute-done.10.b2 = bf16[24,2048]{1,0:T(8,128)(2,1)} collective-permute-done((bf16[24,2048]{1,0:T(8,128)(2,1)}, bf16[24,2048]{1,0:T(8,128)(2,1)}, u32[]{:S(2)}, u32[]{:S(2)}) %collective-permute-start.10) | collective-permute-done | bytes 98336 | tf_op jit(solution)/shard_map/ppermute | solution.py:319
  123.1 4.2 %collective-permute-start.14 = (bf16[24,2048]{1,0:T(8,128)(2,1)S(1)}, bf16[24,2048]{1,0:T(8,128)(2,1)S(1)}, u32[]{:S(2)}, u32[]{:S(2)}) collective-permute-start(bf16[24,2048]{1,0:T(8,128)(2,1)S(1)} %get-tuple-element.71), channel_id=1, source_target_pairs={{0,224},{16,240},{32,192},{48,208},{64,32},{80,48},{96,0},{112,16}... | collective-permute-start | bytes 294920 | tf_op jit(solution)/shard_map/ppermute | solution.py:329
  129.7 7.1 %collective-permute-done.13.p1 = bf16[24,2048]{1,0:T(8,128)(2,1)S(1)} collective-permute-done((bf16[24,2048]{1,0:T(8,128)(2,1)S(1)}, bf16[24,2048]{1,0:T(8,128)(2,1)S(1)}, u32[]{:S(2)}, u32[]{:S(2)}) %collective-permute-start.13) | collective-permute-done | bytes 98336 | tf_op jit(solution)/shard_map/ppermute | solution.py:329
  138.6 7.5 %all-to-all-start.4 = ((bf16[16,16,2048]{2,1,0:T(8,128)(2,1)}), bf16[16,16,2048]{2,1,0:T(8,128)(2,1)}, u32[]{:S(2)}, u32[]{:S(2)}) async-start(bf16[16,16,2048]{2,1,0:T(8,128)(2,1)} %bitcast.59), calls=%async_computation.4 | async-start | bytes 2097152 | tf_op jit(solution)/shard_map/all_to_all | solution.py:338
  149.6 4.4 %collective-permute-done.16.b1 = bf16[24,2048]{1,0:T(8,128)(2,1)S(1)} collective-permute-done((bf16[24,2048]{1,0:T(8,128)(2,1)}, bf16[24,2048]{1,0:T(8,128)(2,1)S(1)}, u32[]{:S(2)}, u32[]{:S(2)}) %collective-permute-start.16) | collective-permute-done | bytes 98336 | tf_op jit(solution)/shard_map/ppermute | solution.py:319
  154.0 3.8 %collective-permute-done.18.b3 = bf16[24,2048]{1,0:T(8,128)(2,1)S(1)} collective-permute-done((bf16[24,2048]{1,0:T(8,128)(2,1)S(1)}, bf16[24,2048]{1,0:T(8,128)(2,1)S(1)}, u32[]{:S(2)}, u32[]{:S(2)}) %collective-permute-start.18) | collective-permute-done | bytes 98336 | tf_op jit(solution)/shard_map/ppermute | solution.py:319
  174.7 7.2 %all-to-all-start.5 = ((bf16[16,16,2048]{2,1,0:T(8,128)(2,1)}), bf16[16,16,2048]{2,1,0:T(8,128)(2,1)S(1)}, u32[]{:S(2)}, u32[]{:S(2)}) async-start(bf16[16,16,2048]{2,1,0:T(8,128)(2,1)} %bitcast.38), calls=%async_computation.5 | async-start | bytes 2097152 | tf_op jit(solution)/shard_map/all_to_all | solution.py:338
  181.9 10.9 %backward.3 = bf16[256,2048]{1,0:T(8,128)(2,1)} custom-call(bf16[256,4096]{1,0:T(8,128)(2,1)} %bitcast.55, bf16[256,2048]{1,0:T(8,128)(2,1)} %bitcast.37.cs, bf16[2048,768]{1,0:T(8,128)(2,1)} %bitcast.70, bf16[2048,768]{1,0:T(8,128)(2,1)} %bitcast.74, bf16[768,2048]{1,0:T(8,128)(2,1)} %bitcast.78), custom_call_target="tpu_custom_call" | custom-call | flops 4026531840 | bytes 13631488 | tf_op jit(solution)/shard_map/backward/pallas_call | solution.py:300
  194.9 5.1 %all-to-all-start.6 = ((bf16[16,16,2048]{2,1,0:T(8,128)(2,1)}), bf16[16,16,2048]{2,1,0:T(8,128)(2,1)S(1)}, u32[]{:S(2)}, u32[]{:S(2)}) async-start(bf16[16,16,2048]{2,1,0:T(8,128)(2,1)} %bitcast.85), calls=%async_computation.6 | async-start | bytes 2097152 | tf_op jit(solution)/shard_map/all_to_all | solution.py:338
  200.1 8.8 %forward.3 = bf16[256,2048]{1,0:T(8,128)(2,1)} custom-call(bf16[256,2048]{1,0:T(8,128)(2,1)} %bitcast.83, bf16[2048,768]{1,0:T(8,128)(2,1)} %bitcast.71, bf16[2048,768]{1,0:T(8,128)(2,1)} %bitcast.75, bf16[768,2048]{1,0:T(8,128)(2,1)} %bitcast.79), custom_call_target="tpu_custom_call" | custom-call | flops 2415919104 | bytes 11534336 | tf_op jit(solution)/shard_map/forward/pallas_call | solution.py:300
  208.8 5.0 %all-to-all-done.6 = bf16[16,16,2048]{2,1,0:T(8,128)(2,1)S(1)} async-done(((bf16[16,16,2048]{2,1,0:T(8,128)(2,1)}), bf16[16,16,2048]{2,1,0:T(8,128)(2,1)S(1)}, u32[]{:S(2)}, u32[]{:S(2)}) %all-to-all-start.6) | async-done | bytes 1048608 | tf_op jit(solution)/shard_map/all_to_all | solution.py:338
  213.9 4.9 %all-to-all-start.7 = ((bf16[16,16,2048]{2,1,0:T(8,128)(2,1)}), bf16[16,16,2048]{2,1,0:T(8,128)(2,1)S(1)}, u32[]{:S(2)}, u32[]{:S(2)}) async-start(bf16[16,16,2048]{2,1,0:T(8,128)(2,1)} %bitcast.81), calls=%async_computation.7 | async-start | bytes 2097152 | tf_op jit(solution)/shard_map/all_to_all | solution.py:338
  225.4 3.8 %collective-permute-done.24.b2 = bf16[24,2048]{1,0:T(8,128)(2,1)S(1)} collective-permute-done((bf16[24,2048]{1,0:T(8,128)(2,1)S(1)}, bf16[24,2048]{1,0:T(8,128)(2,1)S(1)}, u32[]{:S(2)}, u32[]{:S(2)}) %collective-permute-start.24) | collective-permute-done | bytes 98336 | tf_op jit(solution)/shard_map/ppermute | solution.py:319
  (95 shorter events, 88.0 us)
Async XLA Ops:
  2.4 10.4 %collective-permute-start.2 = (bf16[24,4224]{1,0:T(8,128)(2,1)}, bf16[24,4224]{1,0:T(8,128)(2,1)S(1)}, u32[]{:S(2)}, u32[]{:S(2)}) collective-permute-start(bf16[24,4224]{1,0:T(8,128)(2,1)} %pack.1.m0.p0), channel_id=1, source_target_pairs={{0,48},{16,0},{32,16},{48,32},{1,49},{17,1},{33,17},{49,33},{2,50}... | collective-permute-start | bytes 608264 | tf_op jit(solution)/shard_map/ppermute | solution.py:319
  7.0 16.9 %collective-permute-start.1 = (bf16[24,4224]{1,0:T(8,128)(2,1)}, bf16[24,4224]{1,0:T(8,128)(2,1)S(1)}, u32[]{:S(2)}, u32[]{:S(2)}) collective-permute-start(bf16[24,4224]{1,0:T(8,128)(2,1)} %pack.1.m0.p0), channel_id=1, source_target_pairs={{0,32},{16,48},{32,0},{48,16},{1,33},{17,49},{33,1},{49,17},{2,34}... | collective-permute-start | bytes 608264 | tf_op jit(solution)/shard_map/ppermute | solution.py:319
  7.0 16.9 %collective-permute-start = (bf16[24,4224]{1,0:T(8,128)(2,1)}, bf16[24,4224]{1,0:T(8,128)(2,1)S(1)}, u32[]{:S(2)}, u32[]{:S(2)}) collective-permute-start(bf16[24,4224]{1,0:T(8,128)(2,1)} %pack.1.m0.p0), channel_id=1, source_target_pairs={{0,16},{16,32},{32,48},{48,0},{1,17},{17,33},{33,49},{49,1},{2,18}... | collective-permute-start | bytes 608264 | tf_op jit(solution)/shard_map/ppermute | solution.py:319
  28.4 35.9 %all-to-all-start = ((bf16[16,16,4096]{2,1,0:T(8,128)(2,1)}), bf16[16,16,4096]{2,1,0:T(8,128)(2,1)}, u32[]{:S(2)}, u32[]{:S(2)}) async-start(bf16[16,16,4096]{2,1,0:T(8,128)(2,1)} %bitcast.22), calls=%async_computation | async-start | bytes 4194304 | tf_op jit(solution)/shard_map/all_to_all | solution.py:338
  38.0 16.4 %collective-permute-start.4 = (bf16[24,2048]{1,0:T(8,128)(2,1)S(1)}, bf16[24,2048]{1,0:T(8,128)(2,1)S(1)}, u32[]{:S(2)}, u32[]{:S(2)}) collective-permute-start(bf16[24,2048]{1,0:T(8,128)(2,1)S(1)} %bitcast.61), channel_id=1, source_target_pairs={{0,32},{16,48},{32,0},{48,16},{1,33},{17,49},{33,1},{49,17},{2,34}... | collective-permute-start | bytes 294920 | tf_op jit(solution)/shard_map/ppermute | solution.py:319
  40.5 13.9 %collective-permute-start.3 = (bf16[24,2048]{1,0:T(8,128)(2,1)S(1)}, bf16[24,2048]{1,0:T(8,128)(2,1)S(1)}, u32[]{:S(2)}, u32[]{:S(2)}) collective-permute-start(bf16[24,2048]{1,0:T(8,128)(2,1)S(1)} %bitcast.62), channel_id=1, source_target_pairs={{0,16},{16,32},{32,48},{48,0},{1,17},{17,33},{33,49},{49,1},{2,18}... | collective-permute-start | bytes 294920 | tf_op jit(solution)/shard_map/ppermute | solution.py:319
  42.4 13.5 %collective-permute-start.8 = (bf16[24,2048]{1,0:T(8,128)(2,1)S(1)}, bf16[24,2048]{1,0:T(8,128)(2,1)S(1)}, u32[]{:S(2)}, u32[]{:S(2)}) collective-permute-start(bf16[24,2048]{1,0:T(8,128)(2,1)S(1)} %bitcast.64), channel_id=1, source_target_pairs={{0,48},{16,0},{32,16},{48,32},{1,49},{17,1},{33,17},{49,33},{2,50}... | collective-permute-start | bytes 294920 | tf_op jit(solution)/shard_map/ppermute | solution.py:319
  44.3 12.4 %collective-permute-start.7 = (bf16[24,2048]{1,0:T(8,128)(2,1)S(1)}, bf16[24,2048]{1,0:T(8,128)(2,1)S(1)}, u32[]{:S(2)}, u32[]{:S(2)}) collective-permute-start(bf16[24,2048]{1,0:T(8,128)(2,1)S(1)} %bitcast.65), channel_id=1, source_target_pairs={{0,32},{16,48},{32,0},{48,16},{1,33},{17,49},{33,1},{49,17},{2,34}... | collective-permute-start | bytes 294920 | tf_op jit(solution)/shard_map/ppermute | solution.py:319
  44.3 12.4 %collective-permute-start.6 = (bf16[24,2048]{1,0:T(8,128)(2,1)S(1)}, bf16[24,2048]{1,0:T(8,128)(2,1)S(1)}, u32[]{:S(2)}, u32[]{:S(2)}) collective-permute-start(bf16[24,2048]{1,0:T(8,128)(2,1)S(1)} %bitcast.66), channel_id=1, source_target_pairs={{0,16},{16,32},{32,48},{48,0},{1,17},{17,33},{33,49},{49,1},{2,18}... | collective-permute-start | bytes 294920 | tf_op jit(solution)/shard_map/ppermute | solution.py:319
  64.3 18.7 %all-to-all-start.1 = ((bf16[16,16,2048]{2,1,0:T(8,128)(2,1)}), bf16[16,16,2048]{2,1,0:T(8,128)(2,1)S(1)}, u32[]{:S(2)}, u32[]{:S(2)}) async-start(bf16[16,16,2048]{2,1,0:T(8,128)(2,1)} %bitcast.25), calls=%async_computation.1 | async-start | bytes 2097152 | tf_op jit(solution)/shard_map/all_to_all | solution.py:338
  83.0 18.9 %all-to-all-start.2 = ((bf16[16,16,2048]{2,1,0:T(8,128)(2,1)}), bf16[16,16,2048]{2,1,0:T(8,128)(2,1)S(1)}, u32[]{:S(2)}, u32[]{:S(2)}) async-start(bf16[16,16,2048]{2,1,0:T(8,128)(2,1)} %bitcast.84), calls=%async_computation.2 | async-start | bytes 2097152 | tf_op jit(solution)/shard_map/all_to_all | solution.py:338
  102.9 35.7 %all-to-all-start.3 = ((bf16[16,16,4096]{2,1,0:T(8,128)(2,1)}), bf16[16,16,4096]{2,1,0:T(8,128)(2,1)S(1)}, u32[]{:S(2)}, u32[]{:S(2)}) async-start(bf16[16,16,4096]{2,1,0:T(8,128)(2,1)} %bitcast.80), calls=%async_computation.3 | async-start | bytes 4194304 | tf_op jit(solution)/shard_map/all_to_all | solution.py:338
  110.7 9.7 %collective-permute-start.10 = (bf16[24,2048]{1,0:T(8,128)(2,1)}, bf16[24,2048]{1,0:T(8,128)(2,1)}, u32[]{:S(2)}, u32[]{:S(2)}) collective-permute-start(bf16[24,2048]{1,0:T(8,128)(2,1)} %get-tuple-element.67), channel_id=1, source_target_pairs={{0,32},{16,48},{32,0},{48,16},{1,33},{17,49},{33,1},{49,17},{2,34}... | collective-permute-start | bytes 294920 | tf_op jit(solution)/shard_map/ppermute | solution.py:319
  127.3 9.6 %collective-permute-start.13 = (bf16[24,2048]{1,0:T(8,128)(2,1)S(1)}, bf16[24,2048]{1,0:T(8,128)(2,1)S(1)}, u32[]{:S(2)}, u32[]{:S(2)}) collective-permute-start(bf16[24,2048]{1,0:T(8,128)(2,1)S(1)} %get-tuple-element.71), channel_id=1, source_target_pairs={{0,208},{16,224},{32,240},{48,192},{64,16},{80,32},{96,48},{112,0}... | collective-permute-start | bytes 294920 | tf_op jit(solution)/shard_map/ppermute | solution.py:329
  138.6 36.2 %all-to-all-start.4 = ((bf16[16,16,2048]{2,1,0:T(8,128)(2,1)}), bf16[16,16,2048]{2,1,0:T(8,128)(2,1)}, u32[]{:S(2)}, u32[]{:S(2)}) async-start(bf16[16,16,2048]{2,1,0:T(8,128)(2,1)} %bitcast.59), calls=%async_computation.4 | async-start | bytes 2097152 | tf_op jit(solution)/shard_map/all_to_all | solution.py:338
  148.1 9.8 %collective-permute-start.18 = (bf16[24,2048]{1,0:T(8,128)(2,1)S(1)}, bf16[24,2048]{1,0:T(8,128)(2,1)S(1)}, u32[]{:S(2)}, u32[]{:S(2)}) collective-permute-start(bf16[24,2048]{1,0:T(8,128)(2,1)S(1)} %get-tuple-element.78), channel_id=1, source_target_pairs={{0,16},{16,32},{32,48},{48,0},{1,17},{17,33},{33,49},{49,1},{2,18}... | collective-permute-start | bytes 294920 | tf_op jit(solution)/shard_map/ppermute | solution.py:319
  160.8 8.9 %collective-permute-start.21 = (bf16[24,2048]{1,0:T(8,128)(2,1)S(1)}, bf16[24,2048]{1,0:T(8,128)(2,1)S(1)}, u32[]{:S(2)}, u32[]{:S(2)}) collective-permute-start(bf16[24,2048]{1,0:T(8,128)(2,1)S(1)} %get-tuple-element.81), channel_id=1, source_target_pairs={{0,96},{16,112},{32,64},{48,80},{64,160},{80,176},{96,128},{112,14... | collective-permute-start | bytes 294920 | tf_op jit(solution)/shard_map/ppermute | solution.py:329
  162.8 9.5 %collective-permute-start.20 = (bf16[24,2048]{1,0:T(8,128)(2,1)S(1)}, bf16[24,2048]{1,0:T(8,128)(2,1)S(1)}, u32[]{:S(2)}, u32[]{:S(2)}) collective-permute-start(bf16[24,2048]{1,0:T(8,128)(2,1)S(1)} %get-tuple-element.81), channel_id=1, source_target_pairs={{0,80},{16,96},{32,112},{48,64},{64,144},{80,160},{96,176},{112,12... | collective-permute-start | bytes 294920 | tf_op jit(solution)/shard_map/ppermute | solution.py:329
  163.6 9.7 %collective-permute-start.19 = (bf16[24,2048]{1,0:T(8,128)(2,1)S(1)}, bf16[24,2048]{1,0:T(8,128)(2,1)S(1)}, u32[]{:S(2)}, u32[]{:S(2)}) collective-permute-start(bf16[24,2048]{1,0:T(8,128)(2,1)S(1)} %get-tuple-element.81), channel_id=1, source_target_pairs={{0,64},{16,80},{32,96},{48,112},{64,128},{80,144},{96,160},{112,17... | collective-permute-start | bytes 294920 | tf_op jit(solution)/shard_map/ppermute | solution.py:329
  174.7 20.2 %all-to-all-start.5 = ((bf16[16,16,2048]{2,1,0:T(8,128)(2,1)}), bf16[16,16,2048]{2,1,0:T(8,128)(2,1)S(1)}, u32[]{:S(2)}, u32[]{:S(2)}) async-start(bf16[16,16,2048]{2,1,0:T(8,128)(2,1)} %bitcast.38), calls=%async_computation.5 | async-start | bytes 2097152 | tf_op jit(solution)/shard_map/all_to_all | solution.py:338
  194.9 18.9 %all-to-all-start.6 = ((bf16[16,16,2048]{2,1,0:T(8,128)(2,1)}), bf16[16,16,2048]{2,1,0:T(8,128)(2,1)S(1)}, u32[]{:S(2)}, u32[]{:S(2)}) async-start(bf16[16,16,2048]{2,1,0:T(8,128)(2,1)} %bitcast.85), calls=%async_computation.6 | async-start | bytes 2097152 | tf_op jit(solution)/shard_map/all_to_all | solution.py:338
  213.9 19.2 %all-to-all-start.7 = ((bf16[16,16,2048]{2,1,0:T(8,128)(2,1)}), bf16[16,16,2048]{2,1,0:T(8,128)(2,1)S(1)}, u32[]{:S(2)}, u32[]{:S(2)}) async-start(bf16[16,16,2048]{2,1,0:T(8,128)(2,1)} %bitcast.81), calls=%async_computation.7 | async-start | bytes 2097152 | tf_op jit(solution)/shard_map/all_to_all | solution.py:338
  220.3 8.8 %collective-permute-start.24 = (bf16[24,2048]{1,0:T(8,128)(2,1)S(1)}, bf16[24,2048]{1,0:T(8,128)(2,1)S(1)}, u32[]{:S(2)}, u32[]{:S(2)}) collective-permute-start(bf16[24,2048]{1,0:T(8,128)(2,1)S(1)} %get-tuple-element.90), channel_id=1, source_target_pairs={{0,32},{16,48},{32,0},{48,16},{1,33},{17,49},{33,1},{49,17},{2,34}... | collective-permute-start | bytes 294920 | tf_op jit(solution)/shard_map/ppermute | solution.py:319
  234.1 9.0 %collective-permute-start.27 = (bf16[24,2048]{1,0:T(8,128)(2,1)S(1)}, bf16[24,2048]{1,0:T(8,128)(2,1)S(1)}, u32[]{:S(2)}, u32[]{:S(2)}) collective-permute-start(bf16[24,2048]{1,0:T(8,128)(2,1)S(1)} %get-tuple-element.96), channel_id=1, source_target_pairs={{0,32},{16,48},{32,0},{48,16},{1,33},{17,49},{33,1},{49,17},{2,34}... | collective-permute-start | bytes 294920 | tf_op jit(solution)/shard_map/ppermute | solution.py:319
  (26 other events, 180.0 us)

commit v2 on v1

--- a/solution.py
+++ b/solution.py
@@ -521,8 +521,9 @@
     send_x2 = dispatch(3, x_two)
     at_f1 = plane(after(send_f1, at_b1, send_x2))
     back_b1 = plane(after(backward(at_b1, at_b1, 0, 1), at_f1))
-    back_f1 = plane(after(forward(at_f1, send_x2), back_b1))
+    out_f1 = forward(at_f1, send_x2)
     parts_b = combine(1, back_b1)
+    back_f1 = plane(after(out_f1, parts_b[0]))
     grad_one, cot_two = onward(parts_b, section == 0, enter_grad, -1)
     send_c2 = dispatch(3, cot_two)
     at_c2 = plane(after(send_c2, back_f1))

time: 245 us -> 249 us (1.016)
  waiting for transfers between devices: 84.9 us -> 94.9 us
  starting transfers between devices: 92.7 us -> 88.3 us
    all_to_all x8, waiting for transfers between devices: 22.3 us -> 30.2 us  [plane(): lax.all_to_all(block, ('x', 'y'), split_axis=0, concat_axis=0, tiled=True)]
    ppermute x21, starting transfers between devices: 29.5 us -> 25.4 us  [shift(): return lax.ppermute(block, axis, [(i, (i + k) % size) for i in range(size)])]
    unnamed x26 -> x28, local copies, waits for them, and re-layouts: 5.13 us -> 4.83 us
  transfers between devices with their start and end apart: 37 -> 37, of which waited for: 23 -> 22; matrix products, arithmetic and copies ran while one was open for 0% -> 0% of each run, Pallas kernels for 22% -> 21%
where the time goes in v2:
time: 249 us; the launch traced here: 248 us
  waiting for transfers between devices  94.9 us (38%)
  starting transfers between devices  88.3 us (35%)
  Pallas kernels  59.6 us (24%)
  local copies, waits for them, and re-layouts  4.83 us (2%)
    pallas_call x19, Pallas kernels, call(): pl.pallas_call(kernel, name=name, grid=grid, in_specs=in_specs, out_specs...  59.6 us
    ppermute x21, waiting for transfers between devices, shift(): return lax.ppermute(block, axis, [(i, (i + k) % size) for i in range(size)])  50.6 us
    all_to_all x8, starting transfers between devices, plane(): lax.all_to_all(block, ('x', 'y'), split_axis=0, concat_axis=0, tiled=True)  47.4 us
    all_to_all x8, waiting for transfers between devices, plane(): lax.all_to_all(block, ('x', 'y'), split_axis=0, concat_axis=0, tiled=True)  30.2 us
    ppermute x21, starting transfers between devices, shift(): return lax.ppermute(block, axis, [(i, (i + k) % size) for i in range(size)])  25.4 us
    ppermute x8, starting transfers between devices, to_section(): return lax.ppermute(block, ('segment', 'z'), route)  15.5 us
    ppermute x8, waiting for transfers between devices, to_section(): return lax.ppermute(block, ('segment', 'z'), route)  14.1 us
  transfers between devices with their start and end apart: 37, of which 22 were waited for; matrix products, arithmetic and copies ran while one was open for 0% of the time, Pallas kernels for 21%

profile of v2, /device:TPU:8, one launch (start us, length us, event | category | flops | bytes accessed | tf_op | source)
XLA Modules:
  0.0 248.5 jit_solution(9569650261326734717)
XLA Ops:
  2.4 4.6 %collective-permute-start.2 = (bf16[24,4224]{1,0:T(8,128)(2,1)}, bf16[24,4224]{1,0:T(8,128)(2,1)S(1)}, u32[]{:S(2)}, u32[]{:S(2)}) collective-permute-start(bf16[24,4224]{1,0:T(8,128)(2,1)} %pack.1.m0.p0), channel_id=1, source_target_pairs={{0,48},{16,0},{32,16},{48,32},{1,49},{17,1},{33,17},{49,33},{2,50}... | collective-permute-start | bytes 608264 | tf_op jit(solution)/shard_map/ppermute | solution.py:319
  7.7 5.1 %collective-permute-done.2.m3.p3 = bf16[24,4224]{1,0:T(8,128)(2,1)S(1)} collective-permute-done((bf16[24,4224]{1,0:T(8,128)(2,1)}, bf16[24,4224]{1,0:T(8,128)(2,1)S(1)}, u32[]{:S(2)}, u32[]{:S(2)}) %collective-permute-start.2) | collective-permute-done | bytes 202784 | tf_op jit(solution)/shard_map/ppermute | solution.py:319
  12.8 11.1 %collective-permute-done.1.m2.p2 = bf16[24,4224]{1,0:T(8,128)(2,1)S(1)} collective-permute-done((bf16[24,4224]{1,0:T(8,128)(2,1)}, bf16[24,4224]{1,0:T(8,128)(2,1)S(1)}, u32[]{:S(2)}, u32[]{:S(2)}) %collective-permute-start.1) | collective-permute-done | bytes 202784 | tf_op jit(solution)/shard_map/ppermute | solution.py:319
  28.4 7.5 %all-to-all-start = ((bf16[16,16,4096]{2,1,0:T(8,128)(2,1)}), bf16[16,16,4096]{2,1,0:T(8,128)(2,1)}, u32[]{:S(2)}, u32[]{:S(2)}) async-start(bf16[16,16,4096]{2,1,0:T(8,128)(2,1)} %bitcast.22), calls=%async_computation | async-start | bytes 4194304 | tf_op jit(solution)/shard_map/all_to_all | solution.py:338
  47.0 7.4 %collective-permute-done.4.p2 = bf16[24,2048]{1,0:T(8,128)(2,1)S(1)} collective-permute-done((bf16[24,2048]{1,0:T(8,128)(2,1)S(1)}, bf16[24,2048]{1,0:T(8,128)(2,1)S(1)}, u32[]{:S(2)}, u32[]{:S(2)}) %collective-permute-start.4) | collective-permute-done | bytes 98336 | tf_op jit(solution)/shard_map/ppermute | solution.py:319
  58.4 5.9 %all-to-all-done = bf16[16,16,4096]{2,1,0:T(8,128)(2,1)} async-done(((bf16[16,16,4096]{2,1,0:T(8,128)(2,1)}), bf16[16,16,4096]{2,1,0:T(8,128)(2,1)}, u32[]{:S(2)}, u32[]{:S(2)}) %all-to-all-start) | async-done | bytes 2097184 | tf_op jit(solution)/shard_map/all_to_all | solution.py:338
  64.3 5.3 %all-to-all-start.1 = ((bf16[16,16,2048]{2,1,0:T(8,128)(2,1)}), bf16[16,16,2048]{2,1,0:T(8,128)(2,1)S(1)}, u32[]{:S(2)}, u32[]{:S(2)}) async-start(bf16[16,16,2048]{2,1,0:T(8,128)(2,1)} %bitcast.25), calls=%async_computation.1 | async-start | bytes 2097152 | tf_op jit(solution)/shard_map/all_to_all | solution.py:338
  69.6 10.9 %backward.2 = bf16[256,2048]{1,0:T(8,128)(2,1)} custom-call(bf16[256,4096]{1,0:T(8,128)(2,1)} %bitcast.23.xs.cs, bf16[256,4096]{1,0:T(8,128)(2,1)} %bitcast.23.xs.cs, bf16[2048,768]{1,0:T(8,128)(2,1)} %bitcast.68, bf16[2048,768]{1,0:T(8,128)(2,1)} %bitcast.72, bf16[768,2048]{1,0:T(8,128)(2,1)} %bitcast.76), custom_call_target="tpu_custom_call" | custom-call | flops 4026531840 | bytes 14680064 | tf_op jit(solution)/shard_map/backward/pallas_call | solution.py:300
  83.0 4.9 %all-to-all-start.2 = ((bf16[16,16,2048]{2,1,0:T(8,128)(2,1)}), bf16[16,16,2048]{2,1,0:T(8,128)(2,1)S(1)}, u32[]{:S(2)}, u32[]{:S(2)}) async-start(bf16[16,16,2048]{2,1,0:T(8,128)(2,1)} %bitcast.84), calls=%async_computation.2 | async-start | bytes 2097152 | tf_op jit(solution)/shard_map/all_to_all | solution.py:338
  87.9 10.4 %forward.2 = bf16[256,4096]{1,0:T(8,128)(2,1)} custom-call(bf16[256,2048]{1,0:T(8,128)(2,1)} %bitcast.82, bf16[2048,768]{1,0:T(8,128)(2,1)} %bitcast.69, bf16[2048,768]{1,0:T(8,128)(2,1)} %bitcast.73, bf16[768,2048]{1,0:T(8,128)(2,1)} %bitcast.77, bf16[256,2048]{1,0:T(8,128)(2,1)} %copy-done.2), custom_call_target="tpu_custom_call" | custom-call | flops 2415919104 | bytes 13631488 | tf_op jit(solution)/shard_map/forward/pallas_call | solution.py:300
  104.7 5.1 %all-to-all-start.3 = ((bf16[16,16,4096]{2,1,0:T(8,128)(2,1)}), bf16[16,16,4096]{2,1,0:T(8,128)(2,1)S(1)}, u32[]{:S(2)}, u32[]{:S(2)}) async-start(bf16[16,16,4096]{2,1,0:T(8,128)(2,1)} %bitcast.80), calls=%async_computation.3 | async-start | bytes 4194304 | tf_op jit(solution)/shard_map/all_to_all | solution.py:338
  122.2 4.2 %collective-permute-start.14 = (bf16[24,2048]{1,0:T(8,128)(2,1)S(1)}, bf16[24,2048]{1,0:T(8,128)(2,1)S(1)}, u32[]{:S(2)}, u32[]{:S(2)}) collective-permute-start(bf16[24,2048]{1,0:T(8,128)(2,1)S(1)} %get-tuple-element.71), channel_id=1, source_target_pairs={{0,224},{16,240},{32,192},{48,208},{64,32},{80,48},{96,0},{112,16}... | collective-permute-start | bytes 294920 | tf_op jit(solution)/shard_map/ppermute | solution.py:329
  128.9 7.2 %collective-permute-done.13.p1 = bf16[24,2048]{1,0:T(8,128)(2,1)S(1)} collective-permute-done((bf16[24,2048]{1,0:T(8,128)(2,1)S(1)}, bf16[24,2048]{1,0:T(8,128)(2,1)S(1)}, u32[]{:S(2)}, u32[]{:S(2)}) %collective-permute-start.13) | collective-permute-done | bytes 98336 | tf_op jit(solution)/shard_map/ppermute | solution.py:329
  137.8 7.5 %all-to-all-start.4 = ((bf16[16,16,2048]{2,1,0:T(8,128)(2,1)}), bf16[16,16,2048]{2,1,0:T(8,128)(2,1)}, u32[]{:S(2)}, u32[]{:S(2)}) async-start(bf16[16,16,2048]{2,1,0:T(8,128)(2,1)} %bitcast.59), calls=%async_computation.4 | async-start | bytes 2097152 | tf_op jit(solution)/shard_map/all_to_all | solution.py:338
  148.8 4.6 %collective-permute-done.16.b1 = bf16[24,2048]{1,0:T(8,128)(2,1)S(1)} collective-permute-done((bf16[24,2048]{1,0:T(8,128)(2,1)}, bf16[24,2048]{1,0:T(8,128)(2,1)S(1)}, u32[]{:S(2)}, u32[]{:S(2)}) %collective-permute-start.16) | collective-permute-done | bytes 98336 | tf_op jit(solution)/shard_map/ppermute | solution.py:319
  174.0 7.2 %all-to-all-start.5 = ((bf16[16,16,2048]{2,1,0:T(8,128)(2,1)}), bf16[16,16,2048]{2,1,0:T(8,128)(2,1)S(1)}, u32[]{:S(2)}, u32[]{:S(2)}) async-start(bf16[16,16,2048]{2,1,0:T(8,128)(2,1)} %bitcast.38), calls=%async_computation.5 | async-start | bytes 2097152 | tf_op jit(solution)/shard_map/all_to_all | solution.py:338
  181.3 10.9 %backward.3 = bf16[256,2048]{1,0:T(8,128)(2,1)} custom-call(bf16[256,4096]{1,0:T(8,128)(2,1)} %bitcast.55, bf16[256,2048]{1,0:T(8,128)(2,1)} %bitcast.37.cs, bf16[2048,768]{1,0:T(8,128)(2,1)} %bitcast.70, bf16[2048,768]{1,0:T(8,128)(2,1)} %bitcast.74, bf16[768,2048]{1,0:T(8,128)(2,1)} %bitcast.78), custom_call_target="tpu_custom_call" | custom-call | flops 4026531840 | bytes 13631488 | tf_op jit(solution)/shard_map/backward/pallas_call | solution.py:300
  192.1 6.7 %all-to-all-done.5 = bf16[16,16,2048]{2,1,0:T(8,128)(2,1)S(1)} async-done(((bf16[16,16,2048]{2,1,0:T(8,128)(2,1)}), bf16[16,16,2048]{2,1,0:T(8,128)(2,1)S(1)}, u32[]{:S(2)}, u32[]{:S(2)}) %all-to-all-start.5) | async-done | bytes 1048608 | tf_op jit(solution)/shard_map/all_to_all | solution.py:338
  198.9 4.9 %all-to-all-start.6 = ((bf16[16,16,2048]{2,1,0:T(8,128)(2,1)}), bf16[16,16,2048]{2,1,0:T(8,128)(2,1)S(1)}, u32[]{:S(2)}, u32[]{:S(2)}) async-start(bf16[16,16,2048]{2,1,0:T(8,128)(2,1)} %bitcast.85), calls=%async_computation.6 | async-start | bytes 2097152 | tf_op jit(solution)/shard_map/all_to_all | solution.py:338
  203.8 8.8 %forward.3 = bf16[256,2048]{1,0:T(8,128)(2,1)} custom-call(bf16[256,2048]{1,0:T(8,128)(2,1)} %bitcast.83, bf16[2048,768]{1,0:T(8,128)(2,1)} %bitcast.71, bf16[2048,768]{1,0:T(8,128)(2,1)} %bitcast.75, bf16[768,2048]{1,0:T(8,128)(2,1)} %bitcast.79), custom_call_target="tpu_custom_call" | custom-call | flops 2415919104 | bytes 11534336 | tf_op jit(solution)/shard_map/forward/pallas_call | solution.py:300
  212.6 7.4 %all-to-all-done.6 = bf16[16,16,2048]{2,1,0:T(8,128)(2,1)S(1)} async-done(((bf16[16,16,2048]{2,1,0:T(8,128)(2,1)}), bf16[16,16,2048]{2,1,0:T(8,128)(2,1)S(1)}, u32[]{:S(2)}, u32[]{:S(2)}) %all-to-all-start.6) | async-done | bytes 1048608 | tf_op jit(solution)/shard_map/all_to_all | solution.py:338
  219.9 4.9 %all-to-all-start.7 = ((bf16[16,16,2048]{2,1,0:T(8,128)(2,1)}), bf16[16,16,2048]{2,1,0:T(8,128)(2,1)S(1)}, u32[]{:S(2)}, u32[]{:S(2)}) async-start(bf16[16,16,2048]{2,1,0:T(8,128)(2,1)} %bitcast.81), calls=%async_computation.7 | async-start | bytes 2097152 | tf_op jit(solution)/shard_map/all_to_all | solution.py:338
  227.8 4.7 %collective-permute-done.23.b1 = bf16[24,2048]{1,0:T(8,128)(2,1)S(1)} collective-permute-done((bf16[24,2048]{1,0:T(8,128)(2,1)S(1)}, bf16[24,2048]{1,0:T(8,128)(2,1)S(1)}, u32[]{:S(2)}, u32[]{:S(2)}) %collective-permute-start.23) | collective-permute-done | bytes 98336 | tf_op jit(solution)/shard_map/ppermute | solution.py:319
  241.8 4.2 %collective-permute-done.26.b1 = bf16[24,2048]{1,0:T(8,128)(2,1)S(1)} collective-permute-done((bf16[24,2048]{1,0:T(8,128)(2,1)S(1)}, bf16[24,2048]{1,0:T(8,128)(2,1)S(1)}, u32[]{:S(2)}, u32[]{:S(2)}) %collective-permute-start.26) | collective-permute-done | bytes 98336 | tf_op jit(solution)/shard_map/ppermute | solution.py:319
  (97 shorter events, 86.2 us)
Async XLA Ops:
  2.4 10.4 %collective-permute-start.2 = (bf16[24,4224]{1,0:T(8,128)(2,1)}, bf16[24,4224]{1,0:T(8,128)(2,1)S(1)}, u32[]{:S(2)}, u32[]{:S(2)}) collective-permute-start(bf16[24,4224]{1,0:T(8,128)(2,1)} %pack.1.m0.p0), channel_id=1, source_target_pairs={{0,48},{16,0},{32,16},{48,32},{1,49},{17,1},{33,17},{49,33},{2,50}... | collective-permute-start | bytes 608264 | tf_op jit(solution)/shard_map/ppermute | solution.py:319
  7.0 16.9 %collective-permute-start.1 = (bf16[24,4224]{1,0:T(8,128)(2,1)}, bf16[24,4224]{1,0:T(8,128)(2,1)S(1)}, u32[]{:S(2)}, u32[]{:S(2)}) collective-permute-start(bf16[24,4224]{1,0:T(8,128)(2,1)} %pack.1.m0.p0), channel_id=1, source_target_pairs={{0,32},{16,48},{32,0},{48,16},{1,33},{17,49},{33,1},{49,17},{2,34}... | collective-permute-start | bytes 608264 | tf_op jit(solution)/shard_map/ppermute | solution.py:319
  7.0 16.9 %collective-permute-start = (bf16[24,4224]{1,0:T(8,128)(2,1)}, bf16[24,4224]{1,0:T(8,128)(2,1)S(1)}, u32[]{:S(2)}, u32[]{:S(2)}) collective-permute-start(bf16[24,4224]{1,0:T(8,128)(2,1)} %pack.1.m0.p0), channel_id=1, source_target_pairs={{0,16},{16,32},{32,48},{48,0},{1,17},{17,33},{33,49},{49,1},{2,18}... | collective-permute-start | bytes 608264 | tf_op jit(solution)/shard_map/ppermute | solution.py:319
  28.4 35.9 %all-to-all-start = ((bf16[16,16,4096]{2,1,0:T(8,128)(2,1)}), bf16[16,16,4096]{2,1,0:T(8,128)(2,1)}, u32[]{:S(2)}, u32[]{:S(2)}) async-start(bf16[16,16,4096]{2,1,0:T(8,128)(2,1)} %bitcast.22), calls=%async_computation | async-start | bytes 4194304 | tf_op jit(solution)/shard_map/all_to_all | solution.py:338
  38.0 16.4 %collective-permute-start.4 = (bf16[24,2048]{1,0:T(8,128)(2,1)S(1)}, bf16[24,2048]{1,0:T(8,128)(2,1)S(1)}, u32[]{:S(2)}, u32[]{:S(2)}) collective-permute-start(bf16[24,2048]{1,0:T(8,128)(2,1)S(1)} %bitcast.61), channel_id=1, source_target_pairs={{0,32},{16,48},{32,0},{48,16},{1,33},{17,49},{33,1},{49,17},{2,34}... | collective-permute-start | bytes 294920 | tf_op jit(solution)/shard_map/ppermute | solution.py:319
  40.5 13.9 %collective-permute-start.3 = (bf16[24,2048]{1,0:T(8,128)(2,1)S(1)}, bf16[24,2048]{1,0:T(8,128)(2,1)S(1)}, u32[]{:S(2)}, u32[]{:S(2)}) collective-permute-start(bf16[24,2048]{1,0:T(8,128)(2,1)S(1)} %bitcast.62), channel_id=1, source_target_pairs={{0,16},{16,32},{32,48},{48,0},{1,17},{17,33},{33,49},{49,1},{2,18}... | collective-permute-start | bytes 294920 | tf_op jit(solution)/shard_map/ppermute | solution.py:319
  42.4 13.5 %collective-permute-start.8 = (bf16[24,2048]{1,0:T(8,128)(2,1)S(1)}, bf16[24,2048]{1,0:T(8,128)(2,1)S(1)}, u32[]{:S(2)}, u32[]{:S(2)}) collective-permute-start(bf16[24,2048]{1,0:T(8,128)(2,1)S(1)} %bitcast.64), channel_id=1, source_target_pairs={{0,48},{16,0},{32,16},{48,32},{1,49},{17,1},{33,17},{49,33},{2,50}... | collective-permute-start | bytes 294920 | tf_op jit(solution)/shard_map/ppermute | solution.py:319
  44.3 12.4 %collective-permute-start.7 = (bf16[24,2048]{1,0:T(8,128)(2,1)S(1)}, bf16[24,2048]{1,0:T(8,128)(2,1)S(1)}, u32[]{:S(2)}, u32[]{:S(2)}) collective-permute-start(bf16[24,2048]{1,0:T(8,128)(2,1)S(1)} %bitcast.65), channel_id=1, source_target_pairs={{0,32},{16,48},{32,0},{48,16},{1,33},{17,49},{33,1},{49,17},{2,34}... | collective-permute-start | bytes 294920 | tf_op jit(solution)/shard_map/ppermute | solution.py:319
  44.3 12.4 %collective-permute-start.6 = (bf16[24,2048]{1,0:T(8,128)(2,1)S(1)}, bf16[24,2048]{1,0:T(8,128)(2,1)S(1)}, u32[]{:S(2)}, u32[]{:S(2)}) collective-permute-start(bf16[24,2048]{1,0:T(8,128)(2,1)S(1)} %bitcast.66), channel_id=1, source_target_pairs={{0,16},{16,32},{32,48},{48,0},{1,17},{17,33},{33,49},{49,1},{2,18}... | collective-permute-start | bytes 294920 | tf_op jit(solution)/shard_map/ppermute | solution.py:319
  64.3 18.7 %all-to-all-start.1 = ((bf16[16,16,2048]{2,1,0:T(8,128)(2,1)}), bf16[16,16,2048]{2,1,0:T(8,128)(2,1)S(1)}, u32[]{:S(2)}, u32[]{:S(2)}) async-start(bf16[16,16,2048]{2,1,0:T(8,128)(2,1)} %bitcast.25), calls=%async_computation.1 | async-start | bytes 2097152 | tf_op jit(solution)/shard_map/all_to_all | solution.py:338
  83.0 18.9 %all-to-all-start.2 = ((bf16[16,16,2048]{2,1,0:T(8,128)(2,1)}), bf16[16,16,2048]{2,1,0:T(8,128)(2,1)S(1)}, u32[]{:S(2)}, u32[]{:S(2)}) async-start(bf16[16,16,2048]{2,1,0:T(8,128)(2,1)} %bitcast.84), calls=%async_computation.2 | async-start | bytes 2097152 | tf_op jit(solution)/shard_map/all_to_all | solution.py:338
  104.7 33.0 %all-to-all-start.3 = ((bf16[16,16,4096]{2,1,0:T(8,128)(2,1)}), bf16[16,16,4096]{2,1,0:T(8,128)(2,1)S(1)}, u32[]{:S(2)}, u32[]{:S(2)}) async-start(bf16[16,16,4096]{2,1,0:T(8,128)(2,1)} %bitcast.80), calls=%async_computation.3 | async-start | bytes 4194304 | tf_op jit(solution)/shard_map/all_to_all | solution.py:338
  109.8 9.7 %collective-permute-start.10 = (bf16[24,2048]{1,0:T(8,128)(2,1)}, bf16[24,2048]{1,0:T(8,128)(2,1)}, u32[]{:S(2)}, u32[]{:S(2)}) collective-permute-start(bf16[24,2048]{1,0:T(8,128)(2,1)} %copy-done.10), channel_id=1, source_target_pairs={{0,32},{16,48},{32,0},{48,16},{1,33},{17,49},{33,1},{49,17},{2,34}... | collective-permute-start | bytes 294920 | tf_op jit(solution)/shard_map/ppermute | solution.py:319
  126.4 9.7 %collective-permute-start.13 = (bf16[24,2048]{1,0:T(8,128)(2,1)S(1)}, bf16[24,2048]{1,0:T(8,128)(2,1)S(1)}, u32[]{:S(2)}, u32[]{:S(2)}) collective-permute-start(bf16[24,2048]{1,0:T(8,128)(2,1)S(1)} %get-tuple-element.71), channel_id=1, source_target_pairs={{0,208},{16,224},{32,240},{48,192},{64,16},{80,32},{96,48},{112,0}... | collective-permute-start | bytes 294920 | tf_op jit(solution)/shard_map/ppermute | solution.py:329
  137.8 36.3 %all-to-all-start.4 = ((bf16[16,16,2048]{2,1,0:T(8,128)(2,1)}), bf16[16,16,2048]{2,1,0:T(8,128)(2,1)}, u32[]{:S(2)}, u32[]{:S(2)}) async-start(bf16[16,16,2048]{2,1,0:T(8,128)(2,1)} %bitcast.59), calls=%async_computation.4 | async-start | bytes 2097152 | tf_op jit(solution)/shard_map/all_to_all | solution.py:338
  147.2 10.0 %collective-permute-start.18 = (bf16[24,2048]{1,0:T(8,128)(2,1)S(1)}, bf16[24,2048]{1,0:T(8,128)(2,1)S(1)}, u32[]{:S(2)}, u32[]{:S(2)}) collective-permute-start(bf16[24,2048]{1,0:T(8,128)(2,1)S(1)} %get-tuple-element.78), channel_id=1, source_target_pairs={{0,16},{16,32},{32,48},{48,0},{1,17},{17,33},{33,49},{49,1},{2,18}... | collective-permute-start | bytes 294920 | tf_op jit(solution)/shard_map/ppermute | solution.py:319
  160.0 9.7 %collective-permute-start.21 = (bf16[24,2048]{1,0:T(8,128)(2,1)S(1)}, bf16[24,2048]{1,0:T(8,128)(2,1)S(1)}, u32[]{:S(2)}, u32[]{:S(2)}) collective-permute-start(bf16[24,2048]{1,0:T(8,128)(2,1)S(1)} %get-tuple-element.81), channel_id=1, source_target_pairs={{0,96},{16,112},{32,64},{48,80},{64,160},{80,176},{96,128},{112,14... | collective-permute-start | bytes 294920 | tf_op jit(solution)/shard_map/ppermute | solution.py:329
  162.4 8.0 %collective-permute-start.20 = (bf16[24,2048]{1,0:T(8,128)(2,1)S(1)}, bf16[24,2048]{1,0:T(8,128)(2,1)S(1)}, u32[]{:S(2)}, u32[]{:S(2)}) collective-permute-start(bf16[24,2048]{1,0:T(8,128)(2,1)S(1)} %get-tuple-element.81), channel_id=1, source_target_pairs={{0,80},{16,96},{32,112},{48,64},{64,144},{80,160},{96,176},{112,12... | collective-permute-start | bytes 294920 | tf_op jit(solution)/shard_map/ppermute | solution.py:329
  163.8 8.8 %collective-permute-start.19 = (bf16[24,2048]{1,0:T(8,128)(2,1)S(1)}, bf16[24,2048]{1,0:T(8,128)(2,1)S(1)}, u32[]{:S(2)}, u32[]{:S(2)}) collective-permute-start(bf16[24,2048]{1,0:T(8,128)(2,1)S(1)} %get-tuple-element.81), channel_id=1, source_target_pairs={{0,64},{16,80},{32,96},{48,112},{64,128},{80,144},{96,160},{112,17... | collective-permute-start | bytes 294920 | tf_op jit(solution)/shard_map/ppermute | solution.py:329
  174.0 24.8 %all-to-all-start.5 = ((bf16[16,16,2048]{2,1,0:T(8,128)(2,1)}), bf16[16,16,2048]{2,1,0:T(8,128)(2,1)S(1)}, u32[]{:S(2)}, u32[]{:S(2)}) async-start(bf16[16,16,2048]{2,1,0:T(8,128)(2,1)} %bitcast.38), calls=%async_computation.5 | async-start | bytes 2097152 | tf_op jit(solution)/shard_map/all_to_all | solution.py:338
  198.9 21.1 %all-to-all-start.6 = ((bf16[16,16,2048]{2,1,0:T(8,128)(2,1)}), bf16[16,16,2048]{2,1,0:T(8,128)(2,1)S(1)}, u32[]{:S(2)}, u32[]{:S(2)}) async-start(bf16[16,16,2048]{2,1,0:T(8,128)(2,1)} %bitcast.85), calls=%async_computation.6 | async-start | bytes 2097152 | tf_op jit(solution)/shard_map/all_to_all | solution.py:338
  219.9 18.8 %all-to-all-start.7 = ((bf16[16,16,2048]{2,1,0:T(8,128)(2,1)}), bf16[16,16,2048]{2,1,0:T(8,128)(2,1)S(1)}, u32[]{:S(2)}, u32[]{:S(2)}) async-start(bf16[16,16,2048]{2,1,0:T(8,128)(2,1)} %bitcast.81), calls=%async_computation.7 | async-start | bytes 2097152 | tf_op jit(solution)/shard_map/all_to_all | solution.py:338
  225.8 8.1 %collective-permute-start.24 = (bf16[24,2048]{1,0:T(8,128)(2,1)S(1)}, bf16[24,2048]{1,0:T(8,128)(2,1)S(1)}, u32[]{:S(2)}, u32[]{:S(2)}) collective-permute-start(bf16[24,2048]{1,0:T(8,128)(2,1)S(1)} %get-tuple-element.90), channel_id=1, source_target_pairs={{0,32},{16,48},{32,0},{48,16},{1,33},{17,49},{33,1},{49,17},{2,34}... | collective-permute-start | bytes 294920 | tf_op jit(solution)/shard_map/ppermute | solution.py:319
  225.9 8.0 %collective-permute-start.25 = (bf16[24,2048]{1,0:T(8,128)(2,1)S(1)}, bf16[24,2048]{1,0:T(8,128)(2,1)S(1)}, u32[]{:S(2)}, u32[]{:S(2)}) collective-permute-start(bf16[24,2048]{1,0:T(8,128)(2,1)S(1)} %get-tuple-element.91), channel_id=1, source_target_pairs={{0,16},{16,32},{32,48},{48,0},{1,17},{17,33},{33,49},{49,1},{2,18}... | collective-permute-start | bytes 294920 | tf_op jit(solution)/shard_map/ppermute | solution.py:319
  (27 other events, 178.6 us)
